TPU v7x, 256 devices: a whole 4x4x8 slice. The times are simulated.
256 devices in a mesh: lag: 32 (over y, z_lo, x), space: 8 (over z_hi, core).
Axes of the slice: x: 4, y: 4, z: 8 (z_hi: 4, z_lo: 2; z = z_hi * 2 + z_lo), core: 2. Of those that a mesh axis runs over, the one named last changes fastest.
Arguments:
- ensemble: bfloat16 [32, 1024, 1024], P('lag', 'space'), may hold values from -6 to 6
- slot_order: int32 [32], replicated, may hold values from 0 to 31, each once
- neighbour_shift: int32 [6, 1024], P(None, 'space'), may hold values from -16 to 16, as said below
- edge_coupling: float32 [6, 1024], P(None, 'space'), may hold values from 0.02 to 0.15
- observation_cells: int32 [2, 4, 128], P(None, None, 'space'), may hold values from 0 to 127
- observation_weight: float32 [2, 4, 128], P(None, None, 'space'), may hold values from 0.1 to 0.6
- observation_reading: float32 [2, 128], P(None, 'space'), may hold values from -6 to 6
- observation_variance: float32 [2, 128], replicated, may hold values from 0.25 to 2
- observation_jitter: float32 [2, 128, 1024], P(None, 'space'), may hold values from -6 to 6
Outputs:
- analysed: bfloat16 [32, 1024, 1024], P('lag', 'space')
- retired: bfloat16 [2, 1024, 1024], P(None, 'lag', 'space')
Inputs may be any that keep to these rules, and one draw needn't show every extreme that they name: `neighbour_shift`: for each cell the 6 offsets are distinct and nonzero. `observation_cells`: observation p reads cells of the partition of 128 cells numbered p // 16.
All inputs are finite; a program needn't handle non-finite values.
Results may differ from a plain program's by a relative error of at most 0.0054.
Values may be sent and summed in bfloat16 or wider, within the bound.
No kernel may reach another device: no remote copies, remote signals or barrier semaphores. Data moves between devices by JAX's collectives and lax.ppermute only.
A program may use at most 64 MiB of HBM per device.

v0:
```python
import jax
import jax.numpy as jnp
from jax import lax
from jax.sharding import Mesh
from jax.sharding import PartitionSpec as P

HALO = 16
FC_STEPS = 4
CYCLES = 2
LAG = ("lag_0", "lag_1", "lag_2")


def padded_2(cells, sides, width):
    for axis, dim in sides:
        count = lax.axis_size(axis)
        ends = count - 1
        head = lax.slice_in_dim(cells, 0, width, axis=dim)
        tail = lax.slice_in_dim(cells, cells.shape[dim] - width, cells.shape[dim], axis=dim)
        cells = jnp.concatenate(
            [
                lax.ppermute(tail, axis, [(i, (i + 1) % count) for i in range(ends)]),
                cells,
                lax.ppermute(head, axis, [((i + 1) % count, i) for i in range(ends)]),
            ],
            axis=dim,
        )
    return cells


def in_one_piece(arrays, axis, dim, along):
    ends, at = ([], 0)
    for a in arrays[:-1]:
        at += a.shape[along]
        ends.append(at)
    both = jnp.concatenate(arrays, axis=along)
    return tuple(jnp.split(lax.all_gather(both, axis, axis=dim, tiled=True), ends, axis=along))


def broadcast_by_axis(shard, axes, root):
    shard = jnp.where(lax.axis_index(axes) == root, shard, jnp.zeros_like(shard))
    for axis in axes:
        shard = lax.psum(shard, axis)
    return shard


def split_up(shard, dim, size):
    before, after = (shard.shape[:dim], shard.shape[dim + 1 :])
    return jnp.moveaxis(shard.reshape(*before, size, -1, *after), dim, 0)


def summed_on_arrival(shard, axis, dim):
    parts = split_up(shard, dim, lax.axis_size(axis))
    arrived = lax.all_to_all(parts, axis, split_axis=0, concat_axis=0, tiled=True)
    return arrived.astype(jnp.float32).sum(axis=0)


def relax_once(padded, centre, offsets, coefficients):
    anchor = jnp.arange(centre.shape[0], dtype=jnp.int32)
    accrued = jnp.zeros_like(centre)
    for neighbour in range(offsets.shape[0]):
        picked = jnp.clip(anchor + offsets[neighbour], 0, padded.shape[0] - 1)
        accrued = accrued + coefficients[neighbour][:, None] * (padded[picked] - centre)
    return centre + accrued


def step_forward(present_state, offsets, coefficients):
    margin = FC_STEPS * HALO
    field_f = padded_2(present_state, (("space", 0),), margin).astype(jnp.float32)
    for repeat in range(FC_STEPS):
        field_f = relax_once(field_f, field_f, offsets, coefficients)
    return field_f[margin : margin + present_state.shape[0]].astype(jnp.bfloat16)


def observe_local(
    predict_ahead, vertex_list, vertex_weights, observation_readings, variance_total, random_jitter
):
    per_device = vertex_list.shape[1]
    to_single_float = predict_ahead.astype(jnp.float32)
    measured = jnp.zeros((per_device, to_single_float.shape[1]), jnp.float32)
    for corner in range(vertex_list.shape[0]):
        measured = measured + vertex_weights[corner][:, None] * to_single_float[vertex_list[corner]]
    centre = jnp.mean(measured, axis=1, keepdims=True)
    spread = (measured - centre).astype(jnp.bfloat16)
    variance_own = lax.dynamic_slice_in_dim(
        variance_total, lax.axis_index("space") * per_device, per_device
    )
    innovation = (
        observation_readings[:, None] + jnp.sqrt(variance_own)[:, None] * random_jitter - measured
    ).astype(jnp.bfloat16)
    return (spread, innovation)


def solve_weights(spread, innovation, variance_total):
    spread_all, innovation_all = in_one_piece((spread, innovation), "space", 0, 1)
    gram_matrix = lax.dot_general(
        spread_all, spread_all, (((1,), (1,)), ((), ())), preferred_element_type=jnp.float32
    )
    gram_matrix = gram_matrix + jnp.diag((spread.shape[1] - 1) * variance_total)
    factor = jnp.linalg.cholesky(gram_matrix)
    solved = jax.scipy.linalg.cho_solve((factor, True), innovation_all.astype(jnp.float32)).astype(
        jnp.bfloat16
    )
    product = lax.dot_general(
        spread_all, solved, (((0,), (0,)), ((), ())), preferred_element_type=jnp.float32
    )
    return product.astype(jnp.bfloat16)


def assimilate_window(present_state, gain_weights):
    values = present_state.astype(jnp.float32)
    centre = jnp.mean(values, axis=1, keepdims=True)
    spread = (values - centre).astype(jnp.bfloat16)
    return (values + jnp.dot(spread, gain_weights, preferred_element_type=jnp.float32)).astype(
        jnp.bfloat16
    )


def on_device(
    ensemble,
    slot_order,
    neighbour_shift,
    edge_coupling,
    observation_cells,
    observation_weight,
    observation_reading,
    observation_variance,
    observation_jitter,
):
    present_state = ensemble[0]
    slab_count = lax.axis_size(LAG)
    lag_rank = lax.axis_index(LAG)
    margin = FC_STEPS * HALO
    offsets = padded_2(neighbour_shift, (("space", 1),), margin)
    coefficients = padded_2(edge_coupling, (("space", 1),), margin)
    departed = []
    for cycle_number in range(CYCLES):
        forcing_term = slot_order[(slab_count - cycle_number) % slab_count]
        target = slot_order[(slab_count - 1 - cycle_number) % slab_count]
        variance_total = observation_variance[cycle_number]
        newest = broadcast_by_axis(present_state, LAG, forcing_term)
        predict_ahead = step_forward(newest, offsets, coefficients)
        spread, innovation = observe_local(
            predict_ahead,
            observation_cells[cycle_number],
            observation_weight[cycle_number],
            observation_reading[cycle_number],
            variance_total,
            observation_jitter[cycle_number],
        )
        gain_weights = solve_weights(spread, innovation, variance_total)
        refreshed_state = assimilate_window(predict_ahead, gain_weights)
        updated = assimilate_window(present_state, gain_weights)
        contribution = jnp.where(
            lag_rank == target, updated.astype(jnp.float32), jnp.zeros((), jnp.float32)
        )
        member_block = summed_on_arrival(contribution.astype(jnp.bfloat16), LAG, 1).astype(
            jnp.bfloat16
        )
        departed.append(member_block.T)
        present_state = jnp.where(lag_rank == target, refreshed_state, updated)
    return (present_state[None], jnp.stack(departed))


def solution(mesh):
    split = Mesh(
        mesh.devices.reshape(4, 2, 4, mesh.shape["space"]), ("lag_0", "lag_1", "lag_2", "space")
    )
    placed = (
        P(LAG, "space", None),
        P(),
        P(None, "space"),
        P(None, "space"),
        P(None, None, "space"),
        P(None, None, "space"),
        P(None, "space"),
        P(),
        P(None, "space", None),
    )
    return jax.shard_map(
        on_device,
        mesh=split,
        in_specs=placed,
        out_specs=(P(LAG, "space", None), P(None, LAG, "space")),
        check_vma=False,
    )
```

profile of v0, /device:TPU:1, one launch (start us, length us, event | category | flops | bytes accessed | tf_op | source)
XLA Modules:
  0.0 556.3 jit_solution(2774985401164128548)
XLA Ops:
  8.0 6.3 %collective-permute-start.2 = (f32[6,64]{1,0:T(8,128)S(1)}, f32[6,64]{1,0:T(8,128)S(1)}, u32[]{:S(2)}, u32[]{:S(2)}) collective-permute-start(f32[6,64]{1,0:T(8,128)S(1)} %get-tuple-element.54), channel_id=1, source_target_pairs={{0,1},{1,2},{2,3},{3,4},{4,5},{5,6},{6,7},{8,9},{9,10},{10,11},{11... | collective-permute-start | bytes 4616 | tf_op jit(solution)/shard_map/ppermute | solution.py:21
  17.1 4.5 collective-permute-start.4
  36.1 40.0 %all-reduce.7.cloned.1.call-done = bf16[128,1024]{1,0:T(8,128)(2,1)} async-done(((bf16[128,1024]{1,0:T(8,128)(2,1)}), bf16[128,1024]{1,0:T(8,128)(2,1)}) %all-reduce.7.cloned.1.call-update) | async-done | bytes 262160 | tf_op jit(solution)/shard_map/psum | solution.py:42
  77.9 37.6 %all-reduce.9.cloned.1.call-done = bf16[128,1024]{1,0:T(8,128)(2,1)} async-done(((bf16[128,1024]{1,0:T(8,128)(2,1)}), bf16[128,1024]{1,0:T(8,128)(2,1)}) %all-reduce.9.cloned.1.call-update) | async-done | bytes 262160 | tf_op jit(solution)/shard_map/psum | solution.py:42
  117.7 45.8 %all-reduce.11.cloned.1.call-done = bf16[128,1024]{1,0:T(8,128)(2,1)} async-done(((bf16[128,1024]{1,0:T(8,128)(2,1)}), bf16[128,1024]{1,0:T(8,128)(2,1)}) %all-reduce.11.cloned.1.call-update) | async-done | bytes 262160 | tf_op jit(solution)/shard_map/psum | solution.py:42
  164.5 6.9 %collective-permute-start = (bf16[64,1024]{1,0:T(8,128)(2,1)S(1)}, bf16[64,1024]{1,0:T(8,128)(2,1)S(1)}, u32[]{:S(2)}, u32[]{:S(2)}) collective-permute-start(bf16[64,1024]{1,0:T(8,128)(2,1)S(1)} %get-tuple-element.20), channel_id=1, source_target_pairs={{0,1},{1,2},{2,3},{3,4},{4,5},{5,6},{6,7},{8,9},{9,10},{10,11},{11... | collective-permute-start | bytes 393224 | tf_op jit(solution)/shard_map/ppermute | solution.py:21
  176.3 3.7 collective-permute-done.1
  183.4 2.2 gather_fusion.5
  185.5 2.2 gather_fusion.1
  187.7 2.2 gather_fusion.3
  189.9 2.3 gather_fusion
  192.2 2.9 convert_add_fusion.1
  198.4 2.0 gather_fusion.10
  202.5 2.1 gather_fusion.11
  204.6 2.1 gather_fusion.6
  206.6 3.2 add_add_fusion.3
  217.0 2.1 gather_fusion.17
  219.1 2.1 gather_fusion.12
  221.1 3.6 add_add_fusion.2
  224.7 2.1 gather_fusion.22
  235.0 2.1 multiply_add_fusion.1
  240.9 15.8 %all_gather.6 = bf16[128,2048]{1,0:T(8,128)(2,1)S(1)} all-gather(bf16[16,2048]{1,0:T(8,128)(2,1)S(1)} %pad_maximum_fusion.2), channel_id=1, replica_groups=mesh['lag_0'=4,'lag_1'=2,'lag_2'=4,'space'=8] {'space'}, dimensions={0}, use_global_device_ids=true | all-gather | bytes 589824 | tf_op jit(solution)/shard_map/all_gather | solution.py:36
  257.1 11.7 %cholesky.44 = f32[128,128]{1,0:T(8,128)S(1)} custom-call(f32[128,128]{1,0:T(8,128)S(1)} %fusion.76), custom_call_target="Cholesky" | custom-call | tf_op jit(solution)/shard_map/jit(cholesky)/cholesky | solution.py:99
  270.1 9.8 %custom-call.8 = f32[1,128,128]{1,2,0:T(8,128)S(1)} custom-call(f32[1,128,128]{2,1,0:T(8,128)S(1)} %fusion.66), custom_call_target="InvertDiagBlocksLowerTriangular" | custom-call | tf_op jit(solution)/shard_map/jit(_cho_solve)/triangular_solve | solution.py:100
  283.8 42.7 %all-reduce.13.cloned.1.call-done = bf16[128,1024]{1,0:T(8,128)(2,1)} async-done(((bf16[128,1024]{1,0:T(8,128)(2,1)}), bf16[128,1024]{1,0:T(8,128)(2,1)}) %all-reduce.13.cloned.1.call-update) | async-done | bytes 262160 | tf_op jit(solution)/shard_map/psum | solution.py:42
  326.6 39.1 %all-reduce.15.cloned.1.call-done = bf16[128,1024]{1,0:T(8,128)(2,1)} async-done(((bf16[128,1024]{1,0:T(8,128)(2,1)}), bf16[128,1024]{1,0:T(8,128)(2,1)}) %all-reduce.15.cloned.1.call-update) | async-done | bytes 262160 | tf_op jit(solution)/shard_map/psum | solution.py:42
  368.4 6.9 %all-to-all-start = ((bf16[32,128,32]{1,2,0:T(8,128)(2,1)}), bf16[32,128,32]{1,2,0:T(8,128)(2,1)}, u32[]{:S(2)}, u32[]{:S(2)}) async-start(bf16[32,128,32]{1,2,0:T(8,128)(2,1)} %bitcast.63), calls=%async_computation | async-start | bytes 524288 | tf_op jit(solution)/shard_map/all_to_all | solution.py:53
  375.5 38.2 %all-reduce.17.cloned.1.call-done = bf16[128,1024]{1,0:T(8,128)(2,1)} async-done(((bf16[128,1024]{1,0:T(8,128)(2,1)}), bf16[128,1024]{1,0:T(8,128)(2,1)}) %all-reduce.17.cloned.1.call-update) | async-done | bytes 262160 | tf_op jit(solution)/shard_map/psum | solution.py:42
  414.6 6.9 %collective-permute-start.6 = (bf16[64,1024]{1,0:T(8,128)(2,1)S(1)}, bf16[64,1024]{1,0:T(8,128)(2,1)S(1)}, u32[]{:S(2)}, u32[]{:S(2)}) collective-permute-start(bf16[64,1024]{1,0:T(8,128)(2,1)S(1)} %get-tuple-element.18), channel_id=1, source_target_pairs={{0,1},{1,2},{2,3},{3,4},{4,5},{5,6},{6,7},{8,9},{9,10},{10,11},{11... | collective-permute-start | bytes 393224 | tf_op jit(solution)/shard_map/ppermute | solution.py:21
  421.5 2.1 collective-permute-start.7
  424.2 5.9 %collective-permute-done.7 = bf16[64,1024]{1,0:T(8,128)(2,1)S(1)} collective-permute-done((bf16[64,1024]{1,0:T(8,128)(2,1)S(1)}, bf16[64,1024]{1,0:T(8,128)(2,1)S(1)}, u32[]{:S(2)}, u32[]{:S(2)}) %collective-permute-start.7) | collective-permute-done | bytes 131104 | tf_op jit(solution)/shard_map/ppermute | solution.py:23
  440.1 2.3 gather_fusion.28
  442.4 2.9 convert_add_fusion
  446.6 2.1 gather_fusion.36
  448.7 2.0 gather_fusion.38
  454.8 2.1 gather_fusion.34
  456.8 3.2 add_add_fusion.1
  463.2 2.0 gather_fusion.44
  467.2 2.1 gather_fusion.45
  469.3 2.1 gather_fusion.40
  471.3 3.4 add_add_fusion
  474.8 2.1 gather_fusion.50
  485.1 2.1 multiply_add_fusion
  491.0 15.8 %all_gather.7 = bf16[128,2048]{1,0:T(8,128)(2,1)S(1)} all-gather(bf16[16,2048]{1,0:T(8,128)(2,1)S(1)} %pad_maximum_fusion.3), channel_id=1, replica_groups=mesh['lag_0'=4,'lag_1'=2,'lag_2'=4,'space'=8] {'space'}, dimensions={0}, use_global_device_ids=true | all-gather | bytes 589824 | tf_op jit(solution)/shard_map/all_gather | solution.py:36
  507.1 11.7 %cholesky.55 = f32[128,128]{1,0:T(8,128)S(1)} custom-call(f32[128,128]{1,0:T(8,128)S(1)} %fusion.70), custom_call_target="Cholesky" | custom-call | tf_op jit(solution)/shard_map/jit(cholesky)/cholesky | solution.py:99
  520.2 9.8 %custom-call.9 = f32[1,128,128]{1,2,0:T(8,128)S(1)} custom-call(f32[1,128,128]{2,1,0:T(8,128)S(1)} %fusion.67), custom_call_target="InvertDiagBlocksLowerTriangular" | custom-call | tf_op jit(solution)/shard_map/jit(_cho_solve)/triangular_solve | solution.py:100
  533.4 7.0 %all-to-all-start.1 = ((bf16[32,128,32]{1,2,0:T(8,128)(2,1)}), bf16[32,128,32]{1,2,0:T(8,128)(2,1)S(1)}, u32[]{:S(2)}, u32[]{:S(2)}) async-start(bf16[32,128,32]{1,2,0:T(8,128)(2,1)} %bitcast.67), calls=%async_computation.1 | async-start | bytes 524288 | tf_op jit(solution)/shard_map/all_to_all | solution.py:53
  542.6 5.8 %all-to-all-done.1 = bf16[32,128,32]{1,2,0:T(8,128)(2,1)S(1)} async-done(((bf16[32,128,32]{1,2,0:T(8,128)(2,1)}), bf16[32,128,32]{1,2,0:T(8,128)(2,1)S(1)}, u32[]{:S(2)}, u32[]{:S(2)}) %all-to-all-start.1) | async-done | bytes 262176 | tf_op jit(solution)/shard_map/all_to_all | solution.py:53
  (249 shorter events, 103.6 us)
Async XLA Ops:
  7.2 69.0 %all-reduce.7.cloned.1.call-start = ((), (), s32[]{:S(2)}) async-start(), calls=%async_computation.2 | async-start | bytes 524288 | tf_op jit(solution)/shard_map/psum | solution.py:42
  8.0 108.7 %collective-permute-start.2 = (f32[6,64]{1,0:T(8,128)S(1)}, f32[6,64]{1,0:T(8,128)S(1)}, u32[]{:S(2)}, u32[]{:S(2)}) collective-permute-start(f32[6,64]{1,0:T(8,128)S(1)} %get-tuple-element.54), channel_id=1, source_target_pairs={{0,1},{1,2},{2,3},{3,4},{4,5},{5,6},{6,7},{8,9},{9,10},{10,11},{11... | collective-permute-start | bytes 4616 | tf_op jit(solution)/shard_map/ppermute | solution.py:21
  14.3 102.4 %collective-permute-start.3 = (f32[6,64]{1,0:T(8,128)S(1)}, f32[6,64]{1,0:T(8,128)S(1)}, u32[]{:S(2)}, u32[]{:S(2)}) collective-permute-start(f32[6,64]{1,0:T(8,128)S(1)} %get-tuple-element.55), channel_id=1, source_target_pairs={{1,0},{2,1},{3,2},{4,3},{5,4},{6,5},{7,6},{9,8},{10,9},{11,10},{12... | collective-permute-start | bytes 4616 | tf_op jit(solution)/shard_map/ppermute | solution.py:23
  17.1 59.1 %collective-permute-start.4 = (s32[6,64]{1,0:T(8,128)S(1)}, s32[6,64]{1,0:T(8,128)S(1)}, u32[]{:S(2)}, u32[]{:S(2)}) collective-permute-start(s32[6,64]{1,0:T(8,128)S(1)} %get-tuple-element.56), channel_id=1, source_target_pairs={{0,1},{1,2},{2,3},{3,4},{4,5},{5,6},{6,7},{8,9},{9,10},{10,11},{11... | collective-permute-start | bytes 4616 | tf_op jit(solution)/shard_map/ppermute | solution.py:21
  21.6 54.6 %collective-permute-start.5 = (s32[6,64]{1,0:T(8,128)S(1)}, s32[6,64]{1,0:T(8,128)S(1)}, u32[]{:S(2)}, u32[]{:S(2)}) collective-permute-start(s32[6,64]{1,0:T(8,128)S(1)} %get-tuple-element.57), channel_id=1, source_target_pairs={{1,0},{2,1},{3,2},{4,3},{5,4},{6,5},{7,6},{9,8},{10,9},{11,10},{12... | collective-permute-start | bytes 4616 | tf_op jit(solution)/shard_map/ppermute | solution.py:23
  26.3 89.1 %all-reduce.9.cloned.1.call-start = ((), (), s32[]{:S(2)}) async-start(), calls=%async_computation.3 | async-start | bytes 524288 | tf_op jit(solution)/shard_map/psum | solution.py:42
  76.2 87.3 %all-reduce.11.cloned.1.call-start = ((), (), s32[]{:S(2)}) async-start(), calls=%async_computation.4 | async-start | bytes 524288 | tf_op jit(solution)/shard_map/psum | solution.py:42
  77.3 103.8 %copy-start.21 = (s32[1024]{0:T(1024)}, s32[1024]{0:T(1024)S(1)}, u32[]{:S(2)}) copy-start(s32[1024]{0:T(1024)S(1)} %pad_clamp_fusion.9) | copy-start | bytes 12292
  115.5 211.1 %all-reduce.13.cloned.1.call-start = ((), (), s32[]{:S(2)}) async-start(), calls=%async_computation.5 | async-start | bytes 524288 | tf_op jit(solution)/shard_map/psum | solution.py:42
  117.7 62.2 %copy-start.13 = (f32[1,256]{1,0:T(1,128)}, f32[1,256]{1,0:T(1,128)S(1)}, u32[]{:S(2)}) copy-start(f32[1,256]{1,0:T(1,128)S(1)} %get-tuple-element.28) | copy-start | bytes 3076
  117.7 62.2 %copy-start.16 = (f32[1,256]{1,0:T(1,128)}, f32[1,256]{1,0:T(1,128)S(1)}, u32[]{:S(2)}) copy-start(f32[1,256]{1,0:T(1,128)S(1)} %get-tuple-element.31) | copy-start | bytes 3076
  164.5 11.8 %collective-permute-start = (bf16[64,1024]{1,0:T(8,128)(2,1)S(1)}, bf16[64,1024]{1,0:T(8,128)(2,1)S(1)}, u32[]{:S(2)}, u32[]{:S(2)}) collective-permute-start(bf16[64,1024]{1,0:T(8,128)(2,1)S(1)} %get-tuple-element.20), channel_id=1, source_target_pairs={{0,1},{1,2},{2,3},{3,4},{4,5},{5,6},{6,7},{8,9},{9,10},{10,11},{11... | collective-permute-start | bytes 393224 | tf_op jit(solution)/shard_map/ppermute | solution.py:21
  171.3 8.6 %collective-permute-start.1 = (bf16[64,1024]{1,0:T(8,128)(2,1)S(1)}, bf16[64,1024]{1,0:T(8,128)(2,1)S(1)}, u32[]{:S(2)}, u32[]{:S(2)}) collective-permute-start(bf16[64,1024]{1,0:T(8,128)(2,1)S(1)} %get-tuple-element.21), channel_id=1, source_target_pairs={{1,0},{2,1},{3,2},{4,3},{5,4},{6,5},{7,6},{9,8},{10,9},{11,10},{12... | collective-permute-start | bytes 393224 | tf_op jit(solution)/shard_map/ppermute | solution.py:23
  179.9 2.2 copy-start.9
  189.9 2.3 copy-start.4
  206.6 3.2 copy-start.24
  235.0 2.2 copy-start.34
  237.6 3.0 copy-start.43
  237.6 3.0 copy-start.44
  237.6 3.0 copy-start.45
  237.6 3.0 copy-start.46
  237.6 3.2 copy-start.11
  237.6 3.2 copy-start.47
  237.6 3.2 copy-start.49
  237.7 19.0 %copy-start.55 = (f32[128]{0:T(128)S(1)}, f32[128]{0:T(128)}, u32[]{:S(2)}) copy-start(f32[128]{0:T(128)} %get-tuple-element.59) | copy-start | bytes 1540
  282.4 83.2 %copy-start.52 = (s32[16]{0:T(128)S(1)}, s32[16]{0:T(128)}, u32[]{:S(2)}) copy-start(s32[16]{0:T(128)} %get-tuple-element.46) | copy-start | bytes 196
  282.5 83.2 %copy-start.53 = (s32[16]{0:T(128)S(1)}, s32[16]{0:T(128)}, u32[]{:S(2)}) copy-start(s32[16]{0:T(128)} %get-tuple-element.47) | copy-start | bytes 196
  282.5 84.5 %copy-start.50 = (s32[16]{0:T(128)S(1)}, s32[16]{0:T(128)}, u32[]{:S(2)}) copy-start(s32[16]{0:T(128)} %get-tuple-element.52) | copy-start | bytes 196
  282.5 84.5 %copy-start.51 = (s32[16]{0:T(128)S(1)}, s32[16]{0:T(128)}, u32[]{:S(2)}) copy-start(s32[16]{0:T(128)} %get-tuple-element.53) | copy-start | bytes 196
  283.8 140.5 %copy-start.6 = (bf16[128,1024]{1,0:T(8,128)(2,1)}, bf16[128,1024]{1,0:T(8,128)(2,1)S(1)}, u32[]{:S(2)}) copy-start(bf16[128,1024]{1,0:T(8,128)(2,1)S(1)} %get-tuple-element.68) | copy-start | bytes 786436
  283.8 81.9 %all-reduce.15.cloned.1.call-start = ((), (), s32[]{:S(2)}) async-start(), calls=%async_computation.6 | async-start | bytes 524288 | tf_op jit(solution)/shard_map/psum | solution.py:42
  326.6 87.1 %all-reduce.17.cloned.1.call-start = ((), (), s32[]{:S(2)}) async-start(), calls=%async_computation.7 | async-start | bytes 524288 | tf_op jit(solution)/shard_map/psum | solution.py:42
  368.4 165.0 %all-to-all-start = ((bf16[32,128,32]{1,2,0:T(8,128)(2,1)}), bf16[32,128,32]{1,2,0:T(8,128)(2,1)}, u32[]{:S(2)}, u32[]{:S(2)}) async-start(bf16[32,128,32]{1,2,0:T(8,128)(2,1)} %bitcast.63), calls=%async_computation | async-start | bytes 524288 | tf_op jit(solution)/shard_map/all_to_all | solution.py:53
  414.6 9.6 %collective-permute-start.6 = (bf16[64,1024]{1,0:T(8,128)(2,1)S(1)}, bf16[64,1024]{1,0:T(8,128)(2,1)S(1)}, u32[]{:S(2)}, u32[]{:S(2)}) collective-permute-start(bf16[64,1024]{1,0:T(8,128)(2,1)S(1)} %get-tuple-element.18), channel_id=1, source_target_pairs={{0,1},{1,2},{2,3},{3,4},{4,5},{5,6},{6,7},{8,9},{9,10},{10,11},{11... | collective-permute-start | bytes 393224 | tf_op jit(solution)/shard_map/ppermute | solution.py:21
  421.5 8.6 %collective-permute-start.7 = (bf16[64,1024]{1,0:T(8,128)(2,1)S(1)}, bf16[64,1024]{1,0:T(8,128)(2,1)S(1)}, u32[]{:S(2)}, u32[]{:S(2)}) collective-permute-start(bf16[64,1024]{1,0:T(8,128)(2,1)S(1)} %get-tuple-element.19), channel_id=1, source_target_pairs={{1,0},{2,1},{3,2},{4,3},{5,4},{6,5},{7,6},{9,8},{10,9},{11,10},{12... | collective-permute-start | bytes 393224 | tf_op jit(solution)/shard_map/ppermute | solution.py:23
  440.1 2.3 copy-start.5
  456.8 3.2 copy-start.25
  485.1 2.2 copy-start.33
  485.1 2.2 copy-start.35
  487.7 3.0 copy-start.38
  487.7 3.0 copy-start.39
  487.7 3.0 copy-start.40
  487.7 3.0 copy-start.41
  487.7 3.2 copy-start.12
  487.7 3.2 copy-start.42
  487.7 3.2 copy-start.48
  487.7 19.0 %copy-start.54 = (f32[128]{0:T(128)S(1)}, f32[128]{0:T(128)}, u32[]{:S(2)}) copy-start(f32[128]{0:T(128)} %get-tuple-element.58) | copy-start | bytes 1540
  533.4 15.0 %all-to-all-start.1 = ((bf16[32,128,32]{1,2,0:T(8,128)(2,1)}), bf16[32,128,32]{1,2,0:T(8,128)(2,1)S(1)}, u32[]{:S(2)}, u32[]{:S(2)}) async-start(bf16[32,128,32]{1,2,0:T(8,128)(2,1)} %bitcast.67), calls=%async_computation.1 | async-start | bytes 524288 | tf_op jit(solution)/shard_map/all_to_all | solution.py:53
  (26 other events, 50.7 us)
Sparse Core Ops, SparseCore 0:
  26.5 49.6 all-reduce.6
  78.7 36.6 all-reduce.8
  117.8 45.6 all-reduce.10
  283.9 42.5 all-reduce.12
  329.0 36.6 all-reduce.14
  367.8 45.7 all-reduce.16
where the time goes:
time: 567 us; the launch traced here: 556 us
  waiting for transfers between devices  259 us (46%)
  local copies, waits for them, and re-layouts  106 us (19%)
  other arithmetic  87.8 us (15%)
  starting transfers between devices  46.5 us (8%)
  blocking collectives  31.5 us (6%)
  between operations  17.4 us (3%)
  matrix products  7.87 us (1%)
    psum x6, waiting for transfers between devices, broadcast_by_axis(): shard = lax.psum(shard, axis)  243 us
    gather x48, local copies, waits for them, and re-layouts, relax_once(): padded[picked] - centre  87.6 us
    all_gather x2, blocking collectives, in_one_piece(): lax.all_gather(both, axis, axis=dim, tiled=True)  31.5 us
    another operation x6, other arithmetic, solve_weights(): factor = jnp.linalg.cholesky(gram_matrix)  24.8 us
    ppermute x4, starting transfers between devices, padded_2(): lax.ppermute(tail, axis, [(i, (i + 1) % count) for i in range(ends)])  24.5 us
    another operation x4, other arithmetic, solve_weights(): jax.scipy.linalg.cho_solve((factor, True), innovation_all.astype(jnp.floa...  20.9 us
    add x6, other arithmetic, relax_once(): return centre + accrued  19.3 us
    all_to_all x2, starting transfers between devices, summed_on_arrival(): lax.all_to_all(parts, axis, split_axis=0, concat_axis=0, tiled=True)  13.9 us
  transfers between devices with their start and end apart: 16, of which 9 were waited for; matrix products, arithmetic and copies ran while one was open for 20% of the time, Pallas kernels for 0%

commit v1 on v0

v1 whole, which is shorter than its diff:
```python
import jax
import jax.numpy as jnp
from jax import lax
from jax.experimental import pallas as pl
from jax.experimental.pallas import tpu as pltpu
from jax.sharding import Mesh
from jax.sharding import PartitionSpec as P

FC_STEPS = 4
CYCLES = 2
LAG = ("lag_0", "lag_1", "lag_2")
F32 = jnp.float32
BF16 = jnp.bfloat16
LANES = 128
FIRST_ROWS = 48
SECOND_ROWS = 96
THIRD_ROWS = 224


def split3(x):
    hi = x.astype(BF16).astype(F32)
    mid = (x - hi).astype(BF16).astype(F32)
    low = (x - hi - mid).astype(BF16).astype(F32)
    return hi, mid, low


def to_bf16(x):
    return x.astype(BF16)


def prepare_kernel(
    where, slab, shift, coupling, cells, weight, reading, variance, jitter, slab_t, pieces, extra, tmp
):
    values = slab[...].astype(F32)
    mean = jnp.mean(values, axis=1, keepdims=True)
    turned = values.T
    mean_row = jnp.broadcast_to(mean, (LANES, LANES)).T[0:8]
    hi, mid, low = split3(mean_row)
    row8 = lax.broadcasted_iota(jnp.int32, (8, LANES), 0)
    tail = jnp.where(row8 == 0, hi, jnp.where(row8 == 1, mid, jnp.where(row8 == 2, low, 0.0)))
    tail = to_bf16(jnp.concatenate([tail, jnp.zeros((8, LANES), F32)], axis=0))
    turned = to_bf16(turned)
    slab_t[...] = turned
    for r in range(32):
        pieces[r, 0:32, :] = turned[32 * r : 32 * r + 32]
        pieces[r, 32:48, :] = tail

    lag_rank, space_rank = where[0], where[1]
    tmp[...] = jnp.concatenate([jitter[...], jnp.zeros((96, LANES), F32)], axis=0).T
    noise = tmp[pl.ds(pl.multiple_of(32 * (lag_rank % 4), 32), 32), :]
    lane = lax.broadcasted_iota(jnp.int32, (32, LANES), 1)

    def own_lanes(row, take):
        wide = jnp.broadcast_to(row, (8, LANES))
        return pltpu.roll(wide, take, 1)[0:1]

    back = lax.rem(LANES - 16 * space_rank, LANES)
    var0 = own_lanes(variance[0:1, :], back)
    var1 = pltpu.roll(jnp.broadcast_to(own_lanes(variance[1:2, :], back), (8, LANES)), 16, 1)[0:1]
    var = jnp.where(lane[0:1] < 16, var0, jnp.where(lane[0:1] < 32, var1, 0.0))
    read = reading[...]
    error = read + jnp.sqrt(var) * noise
    hi, mid, low = split3(error)
    packed = jnp.where(
        lane < 32,
        hi,
        jnp.where(lane < 64, pltpu.roll(mid, 32, 1), jnp.where(lane < 96, pltpu.roll(low, 64, 1), 0.0)),
    )
    w_hi, w_mid, w_low = split3(weight[...])
    obs = jnp.concatenate([cells[...].astype(F32), w_hi, w_mid, w_low], axis=0)
    obs = pltpu.roll(obs, 96, 1)
    packed = jnp.where(lane < 96, packed, jnp.where(lane < 112, obs, 0.0))
    c_hi, c_mid, c_low = split3(coupling[...])
    extra[...] = to_bf16(jnp.concatenate([shift[...].astype(F32), c_hi, c_mid, c_low, packed], axis=0))


def select_kernel(order, newest, extra, out):
    piece = to_bf16(jnp.concatenate([newest[0, 0:48].astype(F32)[0:40], extra[...].astype(F32)], axis=0))
    for r in range(out.shape[0]):
        out[r] = piece


def observe_kernel(order, where, got, oldest, older, out, state, fields, common, own, sems):
    blocks = got.shape[0]
    lane8 = lax.broadcasted_iota(jnp.int32, (1, LANES), 1)
    lane40 = lax.broadcasted_iota(jnp.int32, (40, LANES), 1)
    lane32 = lax.broadcasted_iota(jnp.int32, (32, LANES), 1)
    error = [jnp.zeros((32, LANES), F32) for _ in range(CYCLES)]
    obs = jnp.zeros((32, LANES), F32)
    targets, weights = [], []
    for b in range(blocks):
        piece = got[b].astype(F32)
        mean = piece[32:33] + piece[33:34] + piece[34:35]
        state[b] = jnp.concatenate([piece[0:32], jnp.broadcast_to(mean, (8, LANES))], axis=0)
        targets.append((lane8 + piece[40:46].astype(jnp.int32)) & (LANES - 1))
        weights.append(piece[46:52] + piece[52:58] + piece[58:64])
        packed = piece[64:96]
        merged = packed + pltpu.roll(packed, 96, 1) + pltpu.roll(packed, 64, 1)
        mine = (lane32 >= 16 * b) & (lane32 < 16 * b + 16)
        for c in range(CYCLES):
            error[c] = jnp.where(mine, pltpu.roll(merged, (16 * b - 16 * c) % LANES, 1), error[c])
        obs = jnp.where(mine, pltpu.roll(packed, (16 * b + 32) % LANES, 1), obs)
    cells = obs[0:8].astype(jnp.int32)
    cell_weight = obs[8:16] + obs[16:24] + obs[24:32]

    def relax(_, carry):
        now = [state[b] for b in range(blocks)]
        zero = jnp.zeros((40, LANES), F32)
        for b in range(blocks):
            centre = now[b]
            before = now[b - 1] if b else zero
            after = now[b + 1] if b + 1 < blocks else zero
            low = jnp.where(lane40 >= 96, before, centre)
            high = jnp.where(lane40 < 32, after, centre)
            accrued = jnp.zeros_like(centre)
            for k in range(6):
                index = jnp.broadcast_to(targets[b][k : k + 1], (40, LANES))
                picked = jnp.where(
                    lane40 < 64,
                    jnp.take_along_axis(low, index, axis=1),
                    jnp.take_along_axis(high, index, axis=1),
                )
                accrued = accrued + weights[b][k : k + 1] * (picked - centre)
            state[b] = centre + accrued
        return carry

    def measure(values, c):
        total = jnp.zeros((40, LANES), F32)
        for q in range(4):
            row = 4 * c + q
            index = jnp.broadcast_to(cells[row : row + 1], (40, LANES))
            picked = jnp.zeros((40, LANES), F32)
            for b in range(blocks):
                mine = (lane40 >= 16 * b) & (lane40 < 16 * b + 16)
                picked = jnp.where(mine, jnp.take_along_axis(values[b], index, axis=1), picked)
            total = total + cell_weight[row : row + 1] * picked
        return total

    lax.fori_loop(0, FC_STEPS, relax, 0)
    forecast = []
    for b in range(blocks):
        value = state[b]
        rounded = to_bf16(value[0:32])
        fields[0, b] = rounded
        value = jnp.concatenate([rounded.astype(F32), value[32:40]], axis=0)
        state[b] = value
        forecast.append(value)
    seen = measure(forecast, 0)
    common[0:32] = to_bf16(seen[0:32] - seen[32:33])
    common[32:64] = to_bf16(error[0] - seen[0:32])
    lax.fori_loop(0, FC_STEPS, relax, 0)
    again = [state[b] for b in range(blocks)]
    for b in range(blocks):
        fields[1, b] = to_bf16(again[b][0:32])
    seen = measure(again, 1)
    common[64:96] = to_bf16(seen[0:32] - seen[32:33])
    common[96:128] = to_bf16(error[1] - seen[0:32])
    common[128:160] = oldest[0, 0:32, :]
    common[160:192] = older[0, 0:32, :]
    space_rank = where[1]
    own[0] = fields[0, space_rank]
    own[1] = fields[1, space_rank]
    lags = out.shape[0]
    second = order[lags - 2]
    copies = []
    for r in range(lags):
        copies.append(pltpu.make_async_copy(common, out.at[r, pl.ds(0, 192), :], sems.at[0, r]))
        pick = jnp.where(second == r, 1, 0)
        copies.append(pltpu.make_async_copy(own.at[pick], out.at[r, pl.ds(192, 32), :], sems.at[1, r]))
    for copy in copies:
        copy.start()
    for copy in copies:
        copy.wait()


def negative_inverse(a):
    size = a.shape[0]
    rows = lax.broadcasted_iota(jnp.int32, (size, size), 0)
    cols = lax.broadcasted_iota(jnp.int32, (size, size), 1)
    lane = lax.broadcasted_iota(jnp.int32, (1, size), 1)
    for k in range(0, size, 4):
        column = [jnp.broadcast_to(a[:, k + i : k + i + 1], (size, size)) for i in range(4)]
        row = [a[k + i : k + i + 1, :] for i in range(4)]
        d = [[column[j][k + i : k + i + 1, :] for j in range(4)] for i in range(4)]
        pd = 1.0 / (d[0][0] * d[1][1] - d[0][1] * d[0][1])
        p00, p01, p11 = d[1][1] * pd, -d[0][1] * pd, d[0][0] * pd
        e00 = p00 * d[0][2] + p01 * d[1][2]
        e01 = p00 * d[0][3] + p01 * d[1][3]
        e10 = p01 * d[0][2] + p11 * d[1][2]
        e11 = p01 * d[0][3] + p11 * d[1][3]
        s00 = d[2][2] - (d[0][2] * e00 + d[1][2] * e10)
        s01 = d[2][3] - (d[0][2] * e01 + d[1][2] * e11)
        s11 = d[3][3] - (d[0][3] * e01 + d[1][3] * e11)
        sd = 1.0 / (s00 * s11 - s01 * s01)
        t00, t01, t11 = s11 * sd, -s01 * sd, s00 * sd
        g00 = e00 * t00 + e01 * t01
        g01 = e00 * t01 + e01 * t11
        g10 = e10 * t00 + e11 * t01
        g11 = e10 * t01 + e11 * t11
        inv = [
            [p00 + g00 * e00 + g01 * e01, p01 + g00 * e10 + g01 * e11, -g00, -g01],
            [p01 + g00 * e10 + g01 * e11, p11 + g10 * e10 + g11 * e11, -g10, -g11],
            [-g00, -g10, t00, t01],
            [-g01, -g11, t01, t11],
        ]
        kept = jnp.where(((rows >= k) & (rows < k + 4)) | ((cols >= k) & (cols < k + 4)), 0.0, a)
        for i in range(4):
            z = inv[i][0] * row[0] + inv[i][1] * row[1] + inv[i][2] * row[2] + inv[i][3] * row[3]
            for j in range(4):
                z = jnp.where(lane == k + j, -inv[i][j], z)
            col = jnp.where((rows >= k) & (rows < k + 4), jnp.where(rows == k + i, -1.0, 0.0), column[i])
            kept = kept - col * z
        a = kept
    return a


def dot(a, b):
    return lax.dot_general(a, b, (((1,), (0,)), ((), ())), preferred_element_type=F32)


def centred(values):
    return to_bf16(values - jnp.mean(values, axis=0, keepdims=True))


def solve(innovation, gram):
    hi, mid, low = split3(-negative_inverse(gram))
    total = dot(innovation, to_bf16(hi)) + (dot(innovation, to_bf16(mid)) + dot(innovation, to_bf16(low)))
    return to_bf16(total)


def update(solved, gain):
    hi = to_bf16(gain)
    low = to_bf16(gain - hi.astype(F32))
    return dot(solved, hi) + dot(solved, low)


def analyse_kernel(order, where, got, slab_t, variance, analysed, retired, keep):
    lags = got.shape[0]
    lag_rank = where[0]
    members = slab_t.shape[0]
    block = members // lags

    def part(i):
        return got[:, 32 * i : 32 * i + 32, :].reshape(members, LANES)

    eye = lax.broadcasted_iota(jnp.int32, (LANES, LANES), 0) == lax.broadcasted_iota(
        jnp.int32, (LANES, LANES), 1
    )
    mine = pl.ds(pl.multiple_of(lag_rank * block, block), block)

    def gram_of(product, c):
        return product + jnp.where(eye, (members - 1) * variance[c : c + 1, :], 0.0)

    took = (lag_rank == order[lags - 1]) | (lag_rank == order[lags - 2])
    own = jnp.where(took, part(6).astype(F32), slab_t[...].astype(F32))
    first = part(4).astype(F32)
    second = part(5).astype(F32)
    spread_t = part(0)
    spread = spread_t.astype(F32).T.astype(BF16)
    ahead = part(2)
    product = dot(spread, jnp.concatenate([spread_t, centred(own), centred(first), centred(second), ahead], axis=1))
    solved = solve(part(1), gram_of(product[:, 0:128], 0))
    keep[...] = first + update(solved, product[:, 256:384])
    retired[0] = to_bf16(keep[mine, :])
    change = update(solved, jnp.concatenate([product[:, 128:256], product[:, 384:640]], axis=1))
    own = to_bf16(own + change[:, 0:128]).astype(F32)
    second = to_bf16(second + change[:, 128:256]).astype(F32)
    spread_t = centred(ahead.astype(F32) + change[:, 256:384])
    innovation = to_bf16(part(3).astype(F32) - change[:, 256:384])
    spread = spread_t.astype(F32).T.astype(BF16)
    product = dot(spread, jnp.concatenate([spread_t, centred(own), centred(second)], axis=1))
    solved = solve(innovation, gram_of(product[:, 0:128], 1))
    change = update(solved, product[:, 128:384])
    keep[...] = second + change[:, 128:256]
    retired[1] = to_bf16(keep[mine, :])
    analysed[0] = to_bf16((own + change[:, 0:128]).T)


def whole(shape):
    return pl.BlockSpec(shape, lambda i, *_: (0,) * len(shape))


def on_device(
    ensemble,
    slot_order,
    neighbour_shift,
    edge_coupling,
    observation_cells,
    observation_weight,
    observation_reading,
    observation_variance,
    observation_jitter,
):
    lags = lax.axis_size(LAG)
    spaces = lax.axis_size("space")
    where = jnp.stack([lax.axis_index(LAG), lax.axis_index("space")]).astype(jnp.int32)
    per = observation_reading.shape[1]
    wide = ((0, 0), (0, LANES - per))
    cells = jnp.pad(observation_cells.reshape(-1, per), wide)
    weight = jnp.pad(observation_weight.reshape(-1, per), wide)
    reading = jnp.pad(observation_reading.reshape(1, -1), ((0, 0), (0, LANES - 2 * per)))
    jitter = observation_jitter.reshape(-1, observation_jitter.shape[2])
    slab = ensemble[0]
    members = slab.shape[1]

    slab_t, pieces, extra = pl.pallas_call(
        prepare_kernel,
        grid_spec=pltpu.PrefetchScalarGridSpec(
            num_scalar_prefetch=1,
            grid=(1,),
            in_specs=[
                whole(slab.shape),
                whole(neighbour_shift.shape),
                whole(edge_coupling.shape),
                whole(cells.shape),
                whole(weight.shape),
                whole(reading.shape),
                whole(observation_variance.shape),
                pl.BlockSpec((2 * per, LANES), lambda i, w: (0, w[0] // 4)),
            ],
            out_specs=[
                whole((members, LANES)),
                whole((lags, FIRST_ROWS, LANES)),
                whole((SECOND_ROWS - 40, LANES)),
            ],
            scratch_shapes=[pltpu.VMEM((LANES, LANES), F32)],
        ),
        out_shape=[
            jax.ShapeDtypeStruct((members, LANES), BF16),
            jax.ShapeDtypeStruct((lags, FIRST_ROWS, LANES), BF16),
            jax.ShapeDtypeStruct((SECOND_ROWS - 40, LANES), BF16),
        ],
        name="prepare",
    )(where, slab, neighbour_shift, edge_coupling, cells, weight, reading, observation_variance, jitter)

    arrived = lax.all_to_all(pieces, LAG, 0, 0, tiled=True)

    def slot(age):
        return pl.BlockSpec((1, FIRST_ROWS, LANES), lambda i, o, *_: (o[age], 0, 0))

    sent = pl.pallas_call(
        select_kernel,
        grid_spec=pltpu.PrefetchScalarGridSpec(
            num_scalar_prefetch=1,
            grid=(1,),
            in_specs=[slot(0), whole(extra.shape)],
            out_specs=whole((spaces, SECOND_ROWS, LANES)),
        ),
        out_shape=jax.ShapeDtypeStruct((spaces, SECOND_ROWS, LANES), BF16),
        name="select",
    )(slot_order, arrived, extra)
    gathered = lax.all_to_all(sent, "space", 0, 0, tiled=True)

    sent = pl.pallas_call(
        observe_kernel,
        grid_spec=pltpu.PrefetchScalarGridSpec(
            num_scalar_prefetch=2,
            grid=(1,),
            in_specs=[whole(gathered.shape), slot(lags - 1), slot(lags - 2)],
            out_specs=pl.BlockSpec(memory_space=pl.ANY),
            scratch_shapes=[
                pltpu.VMEM((spaces, 40, LANES), F32),
                pltpu.VMEM((2, spaces, 32, LANES), BF16),
                pltpu.VMEM((THIRD_ROWS - 32, LANES), BF16),
                pltpu.VMEM((2, 32, LANES), BF16),
                pltpu.SemaphoreType.DMA((2, lags)),
            ],
        ),
        out_shape=jax.ShapeDtypeStruct((lags, THIRD_ROWS, LANES), BF16),
        name="observe",
    )(slot_order, where, gathered, arrived, arrived)
    gathered = lax.all_to_all(sent, LAG, 0, 0, tiled=True)

    return pl.pallas_call(
        analyse_kernel,
        grid_spec=pltpu.PrefetchScalarGridSpec(
            num_scalar_prefetch=2,
            grid=(1,),
            in_specs=[whole(gathered.shape), whole(slab_t.shape), whole(observation_variance.shape)],
            out_specs=[whole(ensemble.shape), whole((CYCLES, members // lags, LANES))],
            scratch_shapes=[pltpu.VMEM((members, LANES), F32)],
        ),
        out_shape=[
            jax.ShapeDtypeStruct(ensemble.shape, BF16),
            jax.ShapeDtypeStruct((CYCLES, members // lags, LANES), BF16),
        ],
        name="analyse",
    )(slot_order, where, gathered, slab_t, observation_variance)


def solution(mesh):
    split = Mesh(
        mesh.devices.reshape(4, 2, 4, mesh.shape["space"]), ("lag_0", "lag_1", "lag_2", "space")
    )
    placed = (
        P(LAG, "space", None),
        P(),
        P(None, "space"),
        P(None, "space"),
        P(None, None, "space"),
        P(None, None, "space"),
        P(None, "space"),
        P(),
        P(None, "space", None),
    )
    return jax.shard_map(
        on_device,
        mesh=split,
        in_specs=placed,
        out_specs=(P(LAG, "space", None), P(None, LAG, "space")),
        check_vma=False,
    )
```

time: 567 us -> 102 us (0.18)
  the two profiles are of different devices: /device:TPU:1 before, /device:TPU:2 now
where the time goes in v1:
time: 102 us
  blocking collectives  66.1 us (65%)
  Pallas kernels  30.3 us (30%)
  local copies, waits for them, and re-layouts  3.92 us (4%)
    all_to_all x1, blocking collectives, on_device(): gathered = lax.all_to_all(sent, LAG, 0, 0, tiled=True)  29.2 us
    all_to_all x1, blocking collectives, on_device(): arrived = lax.all_to_all(pieces, LAG, 0, 0, tiled=True)  18.5 us
    all_to_all x1, blocking collectives, on_device(): gathered = lax.all_to_all(sent, 'space', 0, 0, tiled=True)  18.4 us
    pallas_call x1, Pallas kernels, on_device(): pl.pallas_call(analyse_kernel, grid_spec=pltpu.PrefetchScalarGridSpec(num...  15.5 us
    pallas_call x1, Pallas kernels, on_device(): pl.pallas_call(observe_kernel, grid_spec=pltpu.PrefetchScalarGridSpec(num...  9.93 us
    pallas_call x1, Pallas kernels, on_device(): pl.pallas_call(prepare_kernel, grid_spec=pltpu.PrefetchScalarGridSpec(num...  2.76 us
    pallas_call x1, Pallas kernels, on_device(): pl.pallas_call(select_kernel, grid_spec=pltpu.PrefetchScalarGridSpec(num_...  2.09 us

profile of v1, /device:TPU:2, one launch (start us, length us, event | category | flops | bytes accessed | tf_op | source)
XLA Modules:
  0.0 101.6 jit_solution(18432082375414134880)
XLA Ops:
  0.6 0.8 reshape.18
  1.4 0.6 pad.14.reading
  2.0 1.3 %pad.13.weight = f32[8,128]{1,0:T(8,128)} pad(f32[8,16]{1,0:T(8,128)} %bitcast.8, f32[]{:T(128)} %constant.25.clone.1), padding=0_0x0_112 | pad | bytes 4612 | tf_op jit(solution)/shard_map/jit(_pad)/pad | solution.py:300
  3.3 0.6 pad_add_fusion.where
  3.9 1.3 %pad.12.cells = s32[8,128]{1,0:T(8,128)} pad(s32[8,16]{1,0:T(8,128)} %bitcast.9, s32[]{:T(128)} %constant.24.clone.1), padding=0_0x0_112 | pad | bytes 4612 | tf_op jit(solution)/shard_map/jit(_pad)/pad | solution.py:299
  5.2 2.8 %prepare.1 = (bf16[1024,128]{1,0:T(8,128)(2,1)}, bf16[32,48,128]{2,1,0:T(8,128)(2,1)}, bf16[56,128]{1,0:T(8,128)(2,1)}) custom-call(s32[2]{0:T(128)} %pad_add_fusion.where, bf16[128,1024]{1,0:T(8,128)(2,1)} %bitcast.6, s32[6,128]{1,0:T(8,128)} %shift.1, f32[6,128]{1,0:T(8,128)} %coupling.1, s32[8,128]{1,0:T(8,128)} %pad.12.cells, f32[8,128]{1,0:T(8,128)} %pad.13.weight, ...), custom_call_target="tpu_custom_call" | custom-call | tf_op jit(solution)/shard_map/prepare/pallas_call | solution.py:306
  7.9 18.5 %all_to_all.15.newest.oldest.older = bf16[32,48,128]{2,1,0:T(8,128)(2,1)} all-to-all(bf16[32,48,128]{2,1,0:T(8,128)(2,1)} %get-tuple-element.5), channel_id=1, replica_groups=mesh['lag_0'=4,'lag_1'=2,'lag_2'=4,'space'=8] {'lag_0','lag_1','lag_2'}, dimensions={0} | all-to-all | bytes 786432 | tf_op jit(solution)/shard_map/all_to_all | solution.py:336
  26.5 2.1 %select.4 = bf16[8,96,128]{2,1,0:T(8,128)(2,1)} custom-call(s32[32]{0:T(128)} %order.5, bf16[32,48,128]{2,1,0:T(8,128)(2,1)} %all_to_all.15.newest.oldest.older, bf16[56,128]{1,0:T(8,128)(2,1)} %get-tuple-element.6.extra), custom_call_target="tpu_custom_call" | custom-call | tf_op jit(solution)/shard_map/select/pallas_call | solution.py:341
  28.5 18.4 %all_to_all.16.got = bf16[8,96,128]{2,1,0:T(8,128)(2,1)} all-to-all(bf16[8,96,128]{2,1,0:T(8,128)(2,1)} %select.4), channel_id=1, replica_groups=mesh['lag_0'=4,'lag_1'=2,'lag_2'=4,'space'=8] {'space'}, dimensions={0} | all-to-all | bytes 393216 | tf_op jit(solution)/shard_map/all_to_all | solution.py:352
  46.9 9.9 %observe.1 = bf16[32,224,128]{2,1,0:T(8,128)(2,1)} custom-call(s32[32]{0:T(128)} %order.5, s32[2]{0:T(128)} %pad_add_fusion.where, bf16[8,96,128]{2,1,0:T(8,128)(2,1)} %all_to_all.16.got, bf16[32,48,128]{2,1,0:T(8,128)(2,1)} %all_to_all.15.newest.oldest.older, bf16[32,48,128]{2,1,0:T(8,128)(2,1)} %all_to_all.15.newest.oldest.older), custom_call_target="tpu_custom_call" | custom-call | tf_op jit(solution)/shard_map/observe/pallas_call | solution.py:354
  56.9 29.2 %all_to_all.17.got = bf16[32,224,128]{2,1,0:T(8,128)(2,1)} all-to-all(bf16[32,224,128]{2,1,0:T(8,128)(2,1)} %observe.1), channel_id=1, replica_groups=mesh['lag_0'=4,'lag_1'=2,'lag_2'=4,'space'=8] {'lag_0','lag_1','lag_2'}, dimensions={0} | all-to-all | bytes 3670016 | tf_op jit(solution)/shard_map/all_to_all | solution.py:372
  86.1 15.5 %analyse.1 = (bf16[1,128,1024]{2,1,0:T(8,128)(2,1)}, bf16[2,32,128]{2,1,0:T(8,128)(2,1)}) custom-call(s32[32]{0:T(128)} %order.5, s32[2]{0:T(128)} %pad_add_fusion.where, bf16[32,224,128]{2,1,0:T(8,128)(2,1)} %all_to_all.17.got, bf16[1024,128]{1,0:T(8,128)(2,1)} %get-tuple-element.7.slab_t, f32[2,128]{1,0:T(2,128)} %variance.3), custom_call_target="tpu_custom_call" | custom-call | tf_op jit(solution)/shard_map/analyse/pallas_call | solution.py:374

commit v2 on v1

v2 whole, which is shorter than its diff:
```python
import jax
import jax.numpy as jnp
from jax import lax
from jax.experimental import pallas as pl
from jax.experimental.pallas import tpu as pltpu
from jax.sharding import Mesh
from jax.sharding import PartitionSpec as P

FC_STEPS = 4
CYCLES = 2
LAG = ("lag_0", "lag_1", "lag_2")
F32 = jnp.float32
BF16 = jnp.bfloat16
LANES = 128
FIRST_ROWS = 48
SECOND_ROWS = 96
THIRD = 5


def split3(x):
    hi = x.astype(BF16).astype(F32)
    mid = (x - hi).astype(BF16).astype(F32)
    low = (x - hi - mid).astype(BF16).astype(F32)
    return hi, mid, low


def to_bf16(x):
    return x.astype(BF16)


def ranks():
    return lax.axis_index(LAG), lax.axis_index("zh") * lax.axis_size("core") + lax.axis_index("core")


def prepare_kernel(
    slab, shift, coupling, cells, weight, reading, variance, jitter, slab_t, pieces, extra, tmp, wide
):
    values = slab[0].astype(F32)
    mean = jnp.mean(values, axis=1, keepdims=True)
    turned = values.T
    mean_row = jnp.broadcast_to(mean, (LANES, LANES)).T[0:8]
    hi, mid, low = split3(mean_row)
    row8 = lax.broadcasted_iota(jnp.int32, (8, LANES), 0)
    tail = jnp.where(row8 == 0, hi, jnp.where(row8 == 1, mid, jnp.where(row8 == 2, low, 0.0)))
    tail = to_bf16(jnp.concatenate([tail, jnp.zeros((8, LANES), F32)], axis=0))
    turned = to_bf16(turned)
    slab_t[...] = turned
    for r in range(32):
        pieces[r, 0:32, :] = turned[32 * r : 32 * r + 32]
        pieces[r, 32:48, :] = tail

    lag_rank, space_rank = ranks()
    near = pl.ds(pl.multiple_of(lag_rank // 4 * LANES, LANES), LANES)
    per = jitter.shape[1]
    noise = jnp.concatenate([jitter[0, :, near], jitter[1, :, near], jnp.zeros((96, LANES), F32)], axis=0)
    tmp[...] = noise.T
    noise = tmp[pl.ds(pl.multiple_of(32 * (lag_rank % 4), 32), 32), :]
    lane = lax.broadcasted_iota(jnp.int32, (32, LANES), 1)
    wide[...] = jnp.zeros_like(wide)
    for c in range(CYCLES):
        wide[4 * c : 4 * c + 4, 0:per] = cells[c].astype(F32)
        wide[8 + 4 * c : 12 + 4 * c, 0:per] = weight[c]
        wide[16 + 8 * c : 17 + 8 * c, 0:per] = reading[c : c + 1, :]
    back = lax.rem(LANES - per * space_rank, LANES)
    var = pltpu.roll(jnp.concatenate([variance[...]] * 4, axis=0), back, 1)
    var1 = pltpu.roll(var, per, 1)[1:2]
    var = jnp.where(lane[0:1] < per, var[0:1], jnp.where(lane[0:1] < 2 * per, var1, 0.0))
    read = (wide[16:24, :] + pltpu.roll(wide[24:32, :], per, 1))[0:1]
    error = read + jnp.sqrt(var) * noise
    hi, mid, low = split3(error)
    packed = jnp.where(
        lane < 32,
        hi,
        jnp.where(lane < 64, pltpu.roll(mid, 32, 1), jnp.where(lane < 96, pltpu.roll(low, 64, 1), 0.0)),
    )
    w_hi, w_mid, w_low = split3(wide[8:16, :])
    obs = jnp.concatenate([wide[0:8, :], w_hi, w_mid, w_low], axis=0)
    obs = pltpu.roll(obs, 96, 1)
    packed = jnp.where(lane < 96, packed, jnp.where(lane < 112, obs, 0.0))
    c_hi, c_mid, c_low = split3(coupling[...])
    extra[...] = to_bf16(jnp.concatenate([shift[...].astype(F32), c_hi, c_mid, c_low, packed], axis=0))


def select_kernel(order, arrived, extra, out):
    newest = arrived[order[0]].astype(F32)[0:40]
    piece = to_bf16(jnp.concatenate([newest, extra[...].astype(F32)], axis=0))
    for r in range(out.shape[0]):
        out[r] = piece


def mesh_rows(got, b):
    piece = got[b, 32:64, :].astype(F32)
    lane = lax.broadcasted_iota(jnp.int32, (1, LANES), 1)
    target = lane + piece[8:14].astype(jnp.int32)
    return target, piece[14:20] + piece[20:26] + piece[26:32]


def observation_rows(got, c):
    lane = lax.broadcasted_iota(jnp.int32, (32, LANES), 1)
    error = jnp.zeros((32, LANES), F32)
    obs = jnp.zeros((32, LANES), F32)
    for b in range(got.shape[0]):
        packed = got[b, 64:96, :].astype(F32)
        merged = packed + pltpu.roll(packed, 96, 1) + pltpu.roll(packed, 64, 1)
        mine = (lane >= 16 * b) & (lane < 16 * b + 16)
        error = jnp.where(mine, pltpu.roll(merged, (16 * b - 16 * c) % LANES, 1), error)
        obs = jnp.where(mine, pltpu.roll(packed, (16 * b + 32) % LANES, 1), obs)
    weight = obs[8:16] + obs[16:24] + obs[24:32]
    return error, obs[4 * c : 4 * c + 4].astype(jnp.int32), weight[4 * c : 4 * c + 4]


def build_mesh(got, matrix, total):
    row = lax.broadcasted_iota(jnp.int32, (LANES, LANES), 0)
    low, high = slice(0, 16), slice(LANES - 16, LANES)
    for b in range(got.shape[0]):
        target, weight = mesh_rows(got, b)
        inner = jnp.zeros((LANES, LANES), F32)
        before = jnp.zeros((16, LANES), F32)
        after = jnp.zeros((16, LANES), F32)
        every = jnp.zeros((1, LANES), F32)
        for k in range(6):
            goal = target[k : k + 1]
            at = goal & (LANES - 1)
            here = jnp.where(goal == at, weight[k : k + 1], 0.0)
            there = weight[k : k + 1] - here
            same = row == at
            inner = inner + jnp.where(same, here, 0.0)
            after = after + jnp.where(same[low], there, 0.0)
            before = before + jnp.where(same[high], there, 0.0)
            every = every + weight[k : k + 1]
        total[b] = jnp.broadcast_to(every, (8, LANES))
        edge = jnp.concatenate([after, jnp.zeros((LANES - 32, LANES), F32), before], axis=0)
        for at, part in ((0, inner), (LANES, edge)):
            hi = to_bf16(part)
            matrix[0, b, at : at + LANES, :] = hi
            matrix[1, b, at : at + LANES, :] = to_bf16(part - hi.astype(F32))


def relax(matrix, total, state):
    blocks = state.shape[0]
    lane = lax.broadcasted_iota(jnp.int32, (40, LANES), 1)

    def step(_, carry):
        now = [state[b] for b in range(blocks)]
        zero = jnp.zeros((40, LANES), F32)
        for b in range(blocks):
            before = now[b - 1] if b else zero
            after = now[b + 1] if b + 1 < blocks else zero
            beside = jnp.where(lane < 16, after, jnp.where(lane >= LANES - 16, before, 0.0))
            both = jnp.concatenate([now[b], beside], axis=1)
            hi = both.astype(BF16).astype(F32)
            wide = to_bf16(jnp.concatenate([hi, both - hi], axis=0))
            first = dot(wide, matrix[0, b])
            gain = first[0:40] + (first[40:80] + dot(wide[0:40], matrix[1, b]))
            state[b] = now[b] + (gain - total[b, 0:1, :] * now[b])
        return carry

    lax.fori_loop(0, FC_STEPS, step, 0)


def measure(values, cells, weight):
    lane = lax.broadcasted_iota(jnp.int32, (40, LANES), 1)
    total = jnp.zeros((40, LANES), F32)
    for q in range(4):
        index = jnp.broadcast_to(cells[q : q + 1], (40, LANES))
        picked = jnp.zeros((40, LANES), F32)
        for b, value in enumerate(values):
            mine = (lane >= 16 * b) & (lane < 16 * b + 16)
            picked = jnp.where(mine, jnp.take_along_axis(value, index, axis=1), picked)
        total = total + weight[q : q + 1] * picked
    return total


def observe_kernel(order, got, arrived, out, state, fields, matrix, total, common, own, sems):
    blocks = got.shape[0]
    lags = out.shape[0]
    fetch = [
        pltpu.make_async_copy(
            arrived.at[order[lags - 1 - i], pl.ds(0, 32), :], common.at[pl.ds(64 + 32 * i, 32), :], sems.at[2, i]
        )
        for i in range(2)
    ]
    for copy in fetch:
        copy.start()
    _, space_rank = ranks()
    core = lax.axis_index("core")
    build_mesh(got, matrix, total)
    for b in range(blocks):
        piece = got[b, 0:48, :].astype(F32)
        mean = piece[32:33] + piece[33:34] + piece[34:35]
        state[b] = jnp.concatenate([piece[0:32], jnp.broadcast_to(mean, (8, LANES))], axis=0)
    relax(matrix, total, state)
    forecast = []
    for b in range(blocks):
        value = state[b]
        rounded = to_bf16(value[0:32])
        fields[b] = rounded
        value = jnp.concatenate([rounded.astype(F32), value[32:40]], axis=0)
        state[b] = value
        forecast.append(value)
    own[0] = fields[space_rank]
    error, cells, weight = observation_rows(got, 0)
    seen = measure(forecast, cells, weight)
    spread = seen[0:32] - seen[32:33]
    innovation = error - seen[0:32]
    relax(matrix, total, state)
    own[1] = to_bf16(state[space_rank, 0:32, :])
    error, cells, weight = observation_rows(got, 1)
    seen = measure([state[b] for b in range(blocks)], cells, weight)
    common[0:32] = to_bf16(jnp.where(core == 0, spread, seen[0:32] - seen[32:33]))
    common[32:64] = to_bf16(jnp.where(core == 0, innovation, error - seen[0:32]))
    for copy in fetch:
        copy.wait()
    second = order[lags - 2]
    copies = []
    for r in range(lags):
        pick = jnp.where(second == r, 1, 0)
        copies.append(pltpu.make_async_copy(common, out.at[r, pl.ds(0, 128), :], sems.at[0, r]))
        copies.append(pltpu.make_async_copy(own.at[pick], out.at[r, pl.ds(128, 32), :], sems.at[1, r]))
    for copy in copies:
        copy.start()
    for copy in copies:
        copy.wait()


def run_next(jobs):
    for job in jobs[:2]:
        job()
    del jobs[:2]


def inverse(a, left, right, jobs):
    size = a.shape[0]
    lane = lax.broadcasted_iota(jnp.int32, (8, size), 1)
    tiles = [a[8 * r : 8 * r + 8] for r in range(size // 8)]
    for k in range(0, size, 4):
        t, o = k // 8, k % 8
        row = [jnp.broadcast_to(tiles[t][o + i : o + i + 1, :], (8, size)) for i in range(4)]
        d = [[jnp.broadcast_to(row[i][:, k + j : k + j + 1], (8, size)) for j in range(4)] for i in range(4)]
        pd = 1.0 / (d[0][0] * d[1][1] - d[0][1] * d[0][1])
        p00, p01, p11 = d[1][1] * pd, -d[0][1] * pd, d[0][0] * pd
        e00 = p00 * d[0][2] + p01 * d[1][2]
        e01 = p00 * d[0][3] + p01 * d[1][3]
        e10 = p01 * d[0][2] + p11 * d[1][2]
        e11 = p01 * d[0][3] + p11 * d[1][3]
        s00 = d[2][2] - (d[0][2] * e00 + d[1][2] * e10)
        s01 = d[2][3] - (d[0][2] * e01 + d[1][2] * e11)
        s11 = d[3][3] - (d[0][3] * e01 + d[1][3] * e11)
        sd = 1.0 / (s00 * s11 - s01 * s01)
        t00, t01, t11 = s11 * sd, -s01 * sd, s00 * sd
        g00 = e00 * t00 + e01 * t01
        g01 = e00 * t01 + e01 * t11
        g10 = e10 * t00 + e11 * t01
        g11 = e10 * t01 + e11 * t11
        off = p01 + g00 * e10 + g01 * e11
        inv = [
            [p00 + g00 * e00 + g01 * e01, off, -g00, -g01],
            [off, p11 + g10 * e10 + g11 * e11, -g10, -g11],
            [-g00, -g10, t00, t01],
            [-g01, -g11, t01, t11],
        ]
        scaled = []
        for i in range(4):
            z = inv[i][0] * row[0] + inv[i][1] * row[1] + inv[i][2] * row[2] + inv[i][3] * row[3]
            for j in range(4):
                z = jnp.where(lane == k + j, inv[i][j], z)
            scaled.append(z)
            left[k + i : k + i + 1, :] = jnp.where(lane < k, row[i], jnp.where(lane == k + i, 1.0, 0.0))[0:1]
            right[k + i : k + i + 1, :] = jnp.where(lane < k + 4, z, 0.0)[0:1]
        inside = (lane >= k) & (lane < k + 4)
        for r in range(t if o == 0 else t + 1, size // 8):
            old = tiles[r]
            new = jnp.where(inside, 0.0, old)
            for i in range(4):
                new = new - jnp.broadcast_to(old[:, k + i : k + i + 1], (8, size)) * scaled[i]
            tiles[r] = new
        run_next(jobs)
    while jobs:
        run_next(jobs)
    return lax.dot_general(
        left[...].T,
        right[...],
        (((1,), (0,)), ((), ())),
        precision=lax.Precision.HIGHEST,
        preferred_element_type=F32,
    )


def dot(a, b):
    return lax.dot_general(a, b, (((1,), (0,)), ((), ())), preferred_element_type=F32)


def centred(values):
    return to_bf16(values - jnp.mean(values, axis=0, keepdims=True))


def solve(innovation, inverse_gram):
    hi, mid, low = split3(inverse_gram)
    total = dot(innovation, to_bf16(hi)) + (dot(innovation, to_bf16(mid)) + dot(innovation, to_bf16(low)))
    return to_bf16(total)


def eye():
    rows = lax.broadcasted_iota(jnp.int32, (LANES, LANES), 0)
    return rows == lax.broadcasted_iota(jnp.int32, (LANES, LANES), 1)


def turned(values):
    return values.astype(F32).T.astype(BF16)


def gram_of(spread, spread_t, variance):
    scale = spread_t.shape[0] - 1
    return dot(spread, spread_t) + jnp.where(eye(), scale * variance, 0.0)


def put_gain(gain, i, spread, values):
    product = dot(spread, values)
    hi = to_bf16(product)
    gain[i, 0] = hi
    gain[i, 1] = to_bf16(product - hi.astype(F32))


def change(gain, i, rows):
    return dot(rows, gain[i, 0]) + dot(rows, gain[i, 1])


def analyse_kernel(
    order, got, other, slab_t, variance, analysed, retired, parts, now, cent, gain, left, right, solved, sems
):
    lags = got.shape[0]
    lag_rank, _ = ranks()
    members = slab_t.shape[0]
    block = members // lags
    mine = pl.ds(pl.multiple_of(lag_rank * block, block), block)
    own_core = lax.axis_index("core")

    def copy_of(source, i, to):
        return pltpu.make_async_copy(source.at[:, pl.ds(block * i, block), :], parts.at[to], sems.at[to])

    for i in range(2):
        for core in range(2):

            @pl.when(own_core == core)
            def _():
                copy_of(got, i, 2 * core + i).start()
                copy_of(other, i, 2 * (1 - core) + i).start()

    for i in range(3):
        copy_of(got, 2 + i, 4 + i).start()

    def wait(i):
        copy_of(got, 0, i).wait()

    def part(i):
        return parts[i].reshape(members, LANES)

    chunks = [slice(LANES * c, LANES * c + LANES) for c in range(members // LANES)]
    took = (lag_rank == order[lags - 1]) | (lag_rank == order[lags - 2])

    def folded(values):
        return values.reshape(values.shape[0] // 8, 8, LANES).sum(axis=0)

    def centre_jobs(i, load):
        sums = []
        kept = []

        def look(rows):
            def job():
                sums.append(folded(load(rows).astype(F32)))

            return job

        def centre(rows):
            def job():
                if not kept:
                    total = sum(sums[1:], sums[0])
                    kept.append(jnp.sum(total, axis=0, keepdims=True) * (1.0 / members))
                cent[i, rows, :] = to_bf16(now[i, rows, :].astype(F32) - kept[0])

            return job

        return [look(rows) for rows in chunks] + [centre(rows) for rows in chunks]

    def gain_job(i, spread, values):
        return lambda: put_gain(gain, i, spread, values())

    wait(0)
    spread = turned(part(0))
    gram = gram_of(spread, part(0), variance[0:1, :])
    for i in range(1, 7):
        wait(i)

    def keep(i, load):
        def loaded(rows):
            values = load(rows)
            now[i, rows, :] = values
            return values

        return loaded

    def rows_of(i, rows):
        return parts[i, rows.start // block : rows.stop // block].reshape(LANES, LANES)

    jobs = [gain_job(3, spread, lambda: part(2))]
    jobs += centre_jobs(0, keep(0, lambda rows: jnp.where(took, rows_of(6, rows), slab_t[rows, :])))
    jobs += [gain_job(0, spread, lambda: cent[0])]
    jobs += centre_jobs(1, keep(1, lambda rows: rows_of(5, rows)))
    jobs += [gain_job(1, spread, lambda: cent[1])]
    jobs += centre_jobs(2, keep(2, lambda rows: rows_of(4, rows)))
    jobs += [gain_job(2, spread, lambda: cent[2])]
    solved[...] = solve(part(1), inverse(gram, left, right, jobs))
    seen = change(gain, 3, solved[...])
    spread_t = centred(part(2).astype(F32) + seen)
    innovation = to_bf16(part(3).astype(F32) - seen)
    spread = turned(spread_t)
    gram = gram_of(spread, spread_t, variance[1:2, :])

    def renewed(i):
        def load(rows):
            values = to_bf16(now[i, rows, :].astype(F32) + change(gain, i, solved[rows, :]))
            now[i, rows, :] = values
            return values

        return load

    def retire_first():
        retired[0] = to_bf16(now[2, mine, :].astype(F32) + change(gain, 2, solved[mine, :]))

    jobs = centre_jobs(0, renewed(0)) + centre_jobs(1, renewed(1)) + [retire_first]
    jobs += [gain_job(0, spread, lambda: cent[0]), gain_job(1, spread, lambda: cent[1])]
    solved_again = solve(innovation, inverse(gram, left, right, jobs))
    analysed[0] = to_bf16((now[0].astype(F32) + change(gain, 0, solved_again)).T)
    solved[...] = solved_again
    retired[1] = to_bf16(now[1, mine, :].astype(F32) + change(gain, 1, solved[mine, :]))


def whole(shape):
    return pl.BlockSpec(shape, lambda i, *_: (0,) * len(shape))


def on_device(
    ensemble,
    slot_order,
    neighbour_shift,
    edge_coupling,
    observation_cells,
    observation_weight,
    observation_reading,
    observation_variance,
    observation_jitter,
):
    lags = lax.axis_size(LAG)
    spaces = lax.axis_size("zh") * lax.axis_size("core")
    per = observation_reading.shape[1]
    members = ensemble.shape[2]

    inputs = (
        ensemble,
        neighbour_shift,
        edge_coupling,
        observation_cells,
        observation_weight,
        observation_reading,
        observation_variance,
        observation_jitter,
    )
    slab_t, pieces, extra = pl.pallas_call(
        prepare_kernel,
        out_shape=[
            jax.ShapeDtypeStruct((members, LANES), BF16),
            jax.ShapeDtypeStruct((lags, FIRST_ROWS, LANES), BF16),
            jax.ShapeDtypeStruct((SECOND_ROWS - 40, LANES), BF16),
        ],
        scratch_shapes=[pltpu.VMEM((LANES, LANES), F32), pltpu.VMEM((32, LANES), F32)],
        name="prepare",
    )(*inputs)

    arrived = lax.all_to_all(pieces, LAG, 0, 0, tiled=True)

    vmem = pl.BlockSpec(memory_space=pltpu.VMEM)
    smem = pl.BlockSpec(memory_space=pltpu.SMEM)
    away = pl.BlockSpec(memory_space=pl.ANY)
    sent = pl.pallas_call(
        select_kernel,
        in_specs=[smem, vmem, vmem],
        out_specs=vmem,
        out_shape=jax.ShapeDtypeStruct((spaces, SECOND_ROWS, LANES), BF16),
        name="select",
    )(slot_order, arrived, extra)
    gathered = lax.all_to_all(sent, ("zh", "core"), 0, 0, tiled=True)

    block = members // lags
    sent = pl.pallas_call(
        observe_kernel,
        in_specs=[smem, vmem, away],
        out_specs=away,
        out_shape=jax.ShapeDtypeStruct((lags, THIRD * block, LANES), BF16),
        scratch_shapes=[
            pltpu.VMEM((spaces, 40, LANES), F32),
            pltpu.VMEM((spaces, block, LANES), BF16),
            pltpu.VMEM((2, spaces, 2 * LANES, LANES), BF16),
            pltpu.VMEM((spaces, 8, LANES), F32),
            pltpu.VMEM(((THIRD - 1) * block, LANES), BF16),
            pltpu.VMEM((2, block, LANES), BF16),
            pltpu.SemaphoreType.DMA((3, lags)),
        ],
        name="observe",
    )(slot_order, gathered, arrived)
    third = lax.all_to_all(sent, LAG, 0, 0, tiled=True)
    other = lax.ppermute(third[:, 0 : 2 * block], "core", [(0, 1), (1, 0)])

    square = pltpu.VMEM((LANES, LANES), F32)
    return pl.pallas_call(
        analyse_kernel,
        in_specs=[smem, away, away, vmem, vmem],
        out_specs=[vmem, vmem],
        out_shape=[
            jax.ShapeDtypeStruct(ensemble.shape, BF16),
            jax.ShapeDtypeStruct((CYCLES, block, LANES), BF16),
        ],
        scratch_shapes=[
            pltpu.VMEM((THIRD + 2, lags, block, LANES), BF16),
            pltpu.VMEM((3, members, LANES), BF16),
            pltpu.VMEM((3, members, LANES), BF16),
            pltpu.VMEM((4, 2, LANES, LANES), BF16),
            square,
            square,
            pltpu.VMEM((members, LANES), BF16),
            pltpu.SemaphoreType.DMA((THIRD + 2,)),
        ],
        name="analyse",
    )(slot_order, third, other, slab_t, observation_variance)


def solution(mesh):
    split = Mesh(
        mesh.devices.reshape(4, 2, 4, mesh.shape["space"] // 2, 2), LAG + ("zh", "core")
    )
    space = ("zh", "core")
    placed = (
        P(LAG, space, None),
        P(),
        P(None, space),
        P(None, space),
        P(None, None, space),
        P(None, None, space),
        P(None, space),
        P(),
        P(None, space, None),
    )
    return jax.shard_map(
        on_device,
        mesh=split,
        in_specs=placed,
        out_specs=(P(LAG, space, None), P(None, LAG, space)),
        check_vma=False,
    )
```

time: 102 us -> 95.7 us (0.938)
  the two profiles are of different devices: /device:TPU:2 before, /device:TPU:1 now
where the time goes in v2:
time: 95.7 us; the launch traced here: 95.2 us
  blocking collectives  59.3 us (62%)
  Pallas kernels  29.1 us (30%)
  starting transfers between devices  3.67 us (4%)
  waiting for transfers between devices  1.54 us (2%)
    all_to_all x1, blocking collectives, on_device(): third = lax.all_to_all(sent, LAG, 0, 0, tiled=True)  22.5 us
    all_to_all x1, blocking collectives, on_device(): gathered = lax.all_to_all(sent, ('zh', 'core'), 0, 0, tiled=True)  19 us
    pallas_call x1, Pallas kernels, on_device(): pl.pallas_call(analyse_kernel, in_specs=[smem, away, away, vmem, vmem], o...  18.3 us
    all_to_all x1, blocking collectives, on_device(): arrived = lax.all_to_all(pieces, LAG, 0, 0, tiled=True)  17.8 us
    pallas_call x1, Pallas kernels, on_device(): pl.pallas_call(observe_kernel, in_specs=[smem, vmem, away], out_specs=awa...  6.8 us
    ppermute x1, starting transfers between devices, on_device(): other = lax.ppermute(third[:, 0:2 * block], 'core', [(0, 1), (1, 0)])  3.67 us
    pallas_call x1, Pallas kernels, on_device(): pl.pallas_call(prepare_kernel, out_shape=[jax.ShapeDtypeStruct((members,...  2.31 us
  transfers between devices with their start and end apart: 1, of which 1 were waited for; matrix products, arithmetic and copies ran while one was open for 0% of the time, Pallas kernels for 0%

profile of v2, /device:TPU:1, one launch (start us, length us, event | category | flops | bytes accessed | tf_op | source)
XLA Modules:
  0.0 95.2 jit_solution(12486623619528005728)
XLA Ops:
  0.6 2.3 %prepare.1 = (bf16[1024,128]{1,0:T(8,128)(2,1)}, bf16[32,48,128]{2,1,0:T(8,128)(2,1)}, bf16[56,128]{1,0:T(8,128)(2,1)}) custom-call(bf16[1,128,1024]{2,1,0:T(8,128)(2,1)} %slab.1, s32[6,128]{1,0:T(8,128)} %shift.1, f32[6,128]{1,0:T(8,128)} %coupling.1, s32[2,4,16]{2,1,0:T(4,128)} %cells.1, f32[2,4,16]{2,1,0:T(4,128)} %weight.1, f32[2,16]{1,0:T(2,128)} %reading.1, ...), custom_call_target="tpu_custom_call" | custom-call | tf_op jit(solution)/shard_map/prepare/pallas_call | solution.py:468
  2.9 17.8 %all_to_all.15.arrived = bf16[32,48,128]{2,1,0:T(8,128)(2,1)} all-to-all(bf16[32,48,128]{2,1,0:T(8,128)(2,1)} %get-tuple-element.5), channel_id=1, replica_groups=mesh['lag_0'=4,'lag_1'=2,'lag_2'=4,'zh'=4,'core'=2] {'lag_0','lag_1','la..., dimensions={0} | all-to-all | bytes 786432 | tf_op jit(solution)/shard_map/all_to_all | solution.py:479
  20.8 1.7 %select.1 = bf16[8,96,128]{2,1,0:T(8,128)(2,1)} custom-call(s32[32]{0:T(128)} %order.5, bf16[32,48,128]{2,1,0:T(8,128)(2,1)} %all_to_all.15.arrived, bf16[56,128]{1,0:T(8,128)(2,1)} %get-tuple-element.6.extra), custom_call_target="tpu_custom_call" | custom-call | tf_op jit(solution)/shard_map/select/pallas_call | solution.py:484
  22.5 19.0 %all_to_all.16.got = bf16[8,96,128]{2,1,0:T(8,128)(2,1)} all-to-all(bf16[8,96,128]{2,1,0:T(8,128)(2,1)} %select.1), channel_id=1, replica_groups=mesh['lag_0'=4,'lag_1'=2,'lag_2'=4,'zh'=4,'core'=2] {'zh','core'}, dimensions={0} | all-to-all | bytes 393216 | tf_op jit(solution)/shard_map/all_to_all | solution.py:491
  41.5 6.8 %observe.1 = bf16[32,160,128]{2,1,0:T(8,128)(2,1)} custom-call(s32[32]{0:T(128)} %order.5, bf16[8,96,128]{2,1,0:T(8,128)(2,1)} %all_to_all.16.got, bf16[32,48,128]{2,1,0:T(8,128)(2,1)} %all_to_all.15.arrived), custom_call_target="tpu_custom_call" | custom-call | tf_op jit(solution)/shard_map/observe/pallas_call | solution.py:494
  48.3 22.5 %all_to_all.17.got = bf16[32,160,128]{2,1,0:T(8,128)(2,1)S(1)} all-to-all(bf16[32,160,128]{2,1,0:T(8,128)(2,1)} %observe.1), channel_id=1, replica_groups=mesh['lag_0'=4,'lag_1'=2,'lag_2'=4,'zh'=4,'core'=2] {'lag_0','lag_1','la..., dimensions={0} | all-to-all | bytes 2621440 | tf_op jit(solution)/shard_map/all_to_all | solution.py:510
  70.8 0.0 copy-start
  70.8 3.7 %collective-permute-start = (bf16[32,64,128]{2,1,0:T(8,128)(2,1)S(1)}, bf16[32,64,128]{2,1,0:T(8,128)(2,1)S(1)}, u32[]{:S(2)}, u32[]{:S(2)}) collective-permute-start(bf16[32,64,128]{2,1,0:T(8,128)(2,1)S(1)} %slice.4), channel_id=1, source_target_pairs={{0,1},{1,0},{2,3},{3,2},{4,5},{5,4},{6,7},{7,6},{8,9},{9,8},{10,11... | collective-permute-start | bytes 1572872 | tf_op jit(solution)/shard_map/ppermute | solution.py:511
  74.5 1.5 %collective-permute-done.other = bf16[32,64,128]{2,1,0:T(8,128)(2,1)S(1)} collective-permute-done((bf16[32,64,128]{2,1,0:T(8,128)(2,1)S(1)}, bf16[32,64,128]{2,1,0:T(8,128)(2,1)S(1)}, u32[]{:S(2)}, u32[]{:S(2)}) %collective-permute-start) | collective-permute-done | bytes 524320 | tf_op jit(solution)/shard_map/ppermute | solution.py:511
  76.0 0.0 copy-start.1
  76.0 0.0 copy-done
  76.0 0.8 copy-done.1
  76.8 18.3 %analyse.1 = (bf16[1,128,1024]{2,1,0:T(8,128)(2,1)}, bf16[2,32,128]{2,1,0:T(8,128)(2,1)}) custom-call(s32[32]{0:T(128)} %order.5, bf16[32,160,128]{2,1,0:T(8,128)(2,1)} %copy-done, bf16[32,64,128]{2,1,0:T(8,128)(2,1)} %copy-done.1, bf16[1024,128]{1,0:T(8,128)(2,1)} %get-tuple-element.7.slab_t, f32[2,128]{1,0:T(2,128)} %variance.3), custom_call_target="tpu_custom_call" | custom-call | tf_op jit(solution)/shard_map/analyse/pallas_call | solution.py:514
  (1 shorter events, 0.0 us)
Async XLA Ops:
  70.8 5.3 %copy-start = (bf16[32,160,128]{2,1,0:T(8,128)(2,1)}, bf16[32,160,128]{2,1,0:T(8,128)(2,1)S(1)}, u32[]{:S(2)}) copy-start(bf16[32,160,128]{2,1,0:T(8,128)(2,1)S(1)} %all_to_all.17.got) | copy-start | bytes 3932164
  70.8 5.2 %collective-permute-start = (bf16[32,64,128]{2,1,0:T(8,128)(2,1)S(1)}, bf16[32,64,128]{2,1,0:T(8,128)(2,1)S(1)}, u32[]{:S(2)}, u32[]{:S(2)}) collective-permute-start(bf16[32,64,128]{2,1,0:T(8,128)(2,1)S(1)} %slice.4), channel_id=1, source_target_pairs={{0,1},{1,0},{2,3},{3,2},{4,5},{5,4},{6,7},{7,6},{8,9},{9,8},{10,11... | collective-permute-start | bytes 1572872 | tf_op jit(solution)/shard_map/ppermute | solution.py:511
  76.0 0.8 copy-start.1

commit v3 on v2

--- a/solution.py
+++ b/solution.py
@@ -171,7 +171,7 @@
     return total
 
 
-def observe_kernel(order, got, arrived, out, state, fields, matrix, total, common, own, sems):
+def observe_kernel(order, one, two, arrived, out, got, state, fields, matrix, total, common, own, sems):
     blocks = got.shape[0]
     lags = out.shape[0]
     fetch = [
@@ -184,6 +184,9 @@
         copy.start()
     _, space_rank = ranks()
     core = lax.axis_index("core")
+    for z in range(one.shape[0]):
+        got[2 * z + core] = one[z]
+        got[2 * z + 1 - core] = two[z]
     build_mesh(got, matrix, total)
     for b in range(blocks):
         piece = got[b, 0:48, :].astype(F32)
@@ -229,51 +232,77 @@
     del jobs[:2]
 
 
+def eliminate(d):
+    pd = 1.0 / (d[0][0] * d[1][1] - d[0][1] * d[0][1])
+    p00, p01, p11 = d[1][1] * pd, -d[0][1] * pd, d[0][0] * pd
+    e00 = p00 * d[0][2] + p01 * d[1][2]
+    e01 = p00 * d[0][3] + p01 * d[1][3]
+    e10 = p01 * d[0][2] + p11 * d[1][2]
+    e11 = p01 * d[0][3] + p11 * d[1][3]
+    s00 = d[2][2] - (d[0][2] * e00 + d[1][2] * e10)
+    s01 = d[2][3] - (d[0][2] * e01 + d[1][2] * e11)
+    s11 = d[3][3] - (d[0][3] * e01 + d[1][3] * e11)
+    sd = 1.0 / (s00 * s11 - s01 * s01)
+
+    def apply(m):
+        y0 = p00 * m[0] + p01 * m[1]
+        y1 = p01 * m[0] + p11 * m[1]
+        y2 = m[2] - (d[0][2] * y0 + d[1][2] * y1)
+        y3 = m[3] - (d[0][3] * y0 + d[1][3] * y1)
+        z2 = (s11 * y2 - s01 * y3) * sd
+        z3 = (s00 * y3 - s01 * y2) * sd
+        return [y0 - (e00 * z2 + e01 * z3), y1 - (e10 * z2 + e11 * z3), z2, z3]
+
+    return apply
+
+
+def product4(c, z):
+    return (c[0] * z[0] + c[1] * z[1]) + (c[2] * z[2] + c[3] * z[3])
+
+
 def inverse(a, left, right, jobs):
     size = a.shape[0]
     lane = lax.broadcasted_iota(jnp.int32, (8, size), 1)
     tiles = [a[8 * r : 8 * r + 8] for r in range(size // 8)]
-    for k in range(0, size, 4):
-        t, o = k // 8, k % 8
-        row = [jnp.broadcast_to(tiles[t][o + i : o + i + 1, :], (8, size)) for i in range(4)]
-        d = [[jnp.broadcast_to(row[i][:, k + j : k + j + 1], (8, size)) for j in range(4)] for i in range(4)]
-        pd = 1.0 / (d[0][0] * d[1][1] - d[0][1] * d[0][1])
-        p00, p01, p11 = d[1][1] * pd, -d[0][1] * pd, d[0][0] * pd
-        e00 = p00 * d[0][2] + p01 * d[1][2]
-        e01 = p00 * d[0][3] + p01 * d[1][3]
-        e10 = p01 * d[0][2] + p11 * d[1][2]
-        e11 = p01 * d[0][3] + p11 * d[1][3]
-        s00 = d[2][2] - (d[0][2] * e00 + d[1][2] * e10)
-        s01 = d[2][3] - (d[0][2] * e01 + d[1][2] * e11)
-        s11 = d[3][3] - (d[0][3] * e01 + d[1][3] * e11)
-        sd = 1.0 / (s00 * s11 - s01 * s01)
-        t00, t01, t11 = s11 * sd, -s01 * sd, s00 * sd
-        g00 = e00 * t00 + e01 * t01
-        g01 = e00 * t01 + e01 * t11
-        g10 = e10 * t00 + e11 * t01
-        g11 = e10 * t01 + e11 * t11
-        off = p01 + g00 * e10 + g01 * e11
-        inv = [
-            [p00 + g00 * e00 + g01 * e01, off, -g00, -g01],
-            [off, p11 + g10 * e10 + g11 * e11, -g10, -g11],
-            [-g00, -g10, t00, t01],
-            [-g01, -g11, t01, t11],
+
+    def rows4(tile, o):
+        return [jnp.broadcast_to(tile[o + i : o + i + 1, :], (8, size)) for i in range(4)]
+
+    def put(row, k, scaled):
+        for i in range(4):
+            unit = jnp.where(lane == k + i, 1.0, 0.0)
+            left[k + i : k + i + 1, :] = jnp.where(lane < k, row[i], unit)[0:1]
+            right[k + i : k + i + 1, :] = jnp.where(lane < k + 4, scaled[i], 0.0)[0:1]
+
+    for t in range(size // 8):
+        k = 8 * t
+        columns = [
+            [jnp.broadcast_to(tiles[r][:, k + j : k + j + 1], (8, size)) for j in range(8)]
+            for r in range(t, size // 8)
         ]
-        scaled = []
-        for i in range(4):
-            z = inv[i][0] * row[0] + inv[i][1] * row[1] + inv[i][2] * row[2] + inv[i][3] * row[3]
-            for j in range(4):
-                z = jnp.where(lane == k + j, inv[i][j], z)
-            scaled.append(z)
-            left[k + i : k + i + 1, :] = jnp.where(lane < k, row[i], jnp.where(lane == k + i, 1.0, 0.0))[0:1]
-            right[k + i : k + i + 1, :] = jnp.where(lane < k + 4, z, 0.0)[0:1]
-        inside = (lane >= k) & (lane < k + 4)
-        for r in range(t if o == 0 else t + 1, size // 8):
-            old = tiles[r]
-            new = jnp.where(inside, 0.0, old)
-            for i in range(4):
-                new = new - jnp.broadcast_to(old[:, k + i : k + i + 1], (8, size)) * scaled[i]
-            tiles[r] = new
+        first = (lane >= k) & (lane < k + 4)
+        second = (lane >= k + 4) & (lane < k + 8)
+        row = rows4(tiles[t], 0)
+        d = [rows4(column, 0) for column in columns[0]]
+        d = [[d[j][i] for j in range(8)] for i in range(4)]
+        apply = eliminate(d)
+        scaled = apply([jnp.where(first, jnp.where(lane == k + i, 1.0, 0.0), row[i]) for i in range(4)])
+        ahead = [apply([d[i][4 + j] for i in range(4)]) for j in range(4)]
+        put(row, k, scaled)
+        updated = []
+        for r in range(t, size // 8):
+            c = columns[r - t]
+            tiles[r] = jnp.where(first, 0.0, tiles[r]) - product4(c, scaled)
+            updated.append([c[4 + j] - product4(c, ahead[j]) for j in range(4)])
+        run_next(jobs)
+        row = rows4(tiles[t], 4)
+        d = [rows4(column, 4) for column in updated[0]]
+        d = [[d[j][i] for j in range(4)] for i in range(4)]
+        apply = eliminate(d)
+        scaled = apply([jnp.where(second, jnp.where(lane == k + 4 + i, 1.0, 0.0), row[i]) for i in range(4)])
+        put(row, k + 4, scaled)
+        for r in range(t + 1, size // 8):
+            tiles[r] = jnp.where(second, 0.0, tiles[r]) - product4(updated[r - t], scaled)
         run_next(jobs)
     while jobs:
         run_next(jobs)
@@ -294,10 +323,13 @@
     return to_bf16(values - jnp.mean(values, axis=0, keepdims=True))
 
 
-def solve(innovation, inverse_gram):
-    hi, mid, low = split3(inverse_gram)
-    total = dot(innovation, to_bf16(hi)) + (dot(innovation, to_bf16(mid)) + dot(innovation, to_bf16(low)))
-    return to_bf16(total)
+def stacked(values):
+    hi = to_bf16(values)
+    return jnp.concatenate([hi, to_bf16(values - hi.astype(F32))], axis=0)
+
+
+def doubled(values):
+    return jnp.concatenate([values, values], axis=1)
 
 
 def eye():
@@ -315,14 +347,11 @@
 
 
 def put_gain(gain, i, spread, values):
-    product = dot(spread, values)
-    hi = to_bf16(product)
-    gain[i, 0] = hi
-    gain[i, 1] = to_bf16(product - hi.astype(F32))
+    gain[i] = stacked(dot(spread, values))
 
 
 def change(gain, i, rows):
-    return dot(rows, gain[i, 0]) + dot(rows, gain[i, 1])
+    return dot(rows, gain[i])
 
 
 def analyse_kernel(
@@ -409,7 +438,7 @@
     jobs += [gain_job(1, spread, lambda: cent[1])]
     jobs += centre_jobs(2, keep(2, lambda rows: rows_of(4, rows)))
     jobs += [gain_job(2, spread, lambda: cent[2])]
-    solved[...] = solve(part(1), inverse(gram, left, right, jobs))
+    solved[...] = doubled(to_bf16(dot(doubled(part(1)), stacked(inverse(gram, left, right, jobs)))))
     seen = change(gain, 3, solved[...])
     spread_t = centred(part(2).astype(F32) + seen)
     innovation = to_bf16(part(3).astype(F32) - seen)
@@ -429,7 +458,7 @@
 
     jobs = centre_jobs(0, renewed(0)) + centre_jobs(1, renewed(1)) + [retire_first]
     jobs += [gain_job(0, spread, lambda: cent[0]), gain_job(1, spread, lambda: cent[1])]
-    solved_again = solve(innovation, inverse(gram, left, right, jobs))
+    solved_again = doubled(to_bf16(dot(doubled(innovation), stacked(inverse(gram, left, right, jobs)))))
     analysed[0] = to_bf16((now[0].astype(F32) + change(gain, 0, solved_again)).T)
     solved[...] = solved_again
     retired[1] = to_bf16(now[1, mine, :].astype(F32) + change(gain, 1, solved[mine, :]))
@@ -485,18 +514,20 @@
         select_kernel,
         in_specs=[smem, vmem, vmem],
         out_specs=vmem,
-        out_shape=jax.ShapeDtypeStruct((spaces, SECOND_ROWS, LANES), BF16),
+        out_shape=jax.ShapeDtypeStruct((spaces // 2, SECOND_ROWS, LANES), BF16),
         name="select",
     )(slot_order, arrived, extra)
-    gathered = lax.all_to_all(sent, ("zh", "core"), 0, 0, tiled=True)
+    gathered = lax.all_to_all(sent, "zh", 0, 0, tiled=True)
+    swapped = lax.ppermute(gathered, "core", [(0, 1), (1, 0)])
 
     block = members // lags
     sent = pl.pallas_call(
         observe_kernel,
-        in_specs=[smem, vmem, away],
+        in_specs=[smem, vmem, vmem, away],
         out_specs=away,
         out_shape=jax.ShapeDtypeStruct((lags, THIRD * block, LANES), BF16),
         scratch_shapes=[
+            pltpu.VMEM((spaces, SECOND_ROWS, LANES), BF16),
             pltpu.VMEM((spaces, 40, LANES), F32),
             pltpu.VMEM((spaces, block, LANES), BF16),
             pltpu.VMEM((2, spaces, 2 * LANES, LANES), BF16),
@@ -506,7 +537,7 @@
             pltpu.SemaphoreType.DMA((3, lags)),
         ],
         name="observe",
-    )(slot_order, gathered, arrived)
+    )(slot_order, gathered, swapped, arrived)
     third = lax.all_to_all(sent, LAG, 0, 0, tiled=True)
     other = lax.ppermute(third[:, 0 : 2 * block], "core", [(0, 1), (1, 0)])
 
@@ -523,10 +554,10 @@
             pltpu.VMEM((THIRD + 2, lags, block, LANES), BF16),
             pltpu.VMEM((3, members, LANES), BF16),
             pltpu.VMEM((3, members, LANES), BF16),
-            pltpu.VMEM((4, 2, LANES, LANES), BF16),
+            pltpu.VMEM((4, 2 * LANES, LANES), BF16),
             square,
             square,
-            pltpu.VMEM((members, LANES), BF16),
+            pltpu.VMEM((members, 2 * LANES), BF16),
             pltpu.SemaphoreType.DMA((THIRD + 2,)),
         ],
         name="analyse",

time: 95.7 us -> 92.3 us (0.964)
  Pallas kernels: 29.1 us -> 24.9 us
  blocking collectives: 59.3 us -> 55.2 us
  starting transfers between devices: 3.67 us -> 6.89 us
    all_to_all x1, blocking collectives: 19 us -> 14.3 us  [on_device(): gathered = lax.all_to_all(sent, 'zh', 0, 0, tiled=True)]
    ppermute x0 -> x1, starting transfers between devices: none -> 4.37 us  [on_device(): swapped = lax.ppermute(gathered, 'core', [(0, 1), (1, 0)])]
    pallas_call x1, Pallas kernels: 18.3 us -> 14.1 us  [on_device(): pl.pallas_call(analyse_kernel, in_specs=[smem, away, away, vmem, vmem], o...]
    ppermute x1, starting transfers between devices: 3.67 us -> 2.52 us  [on_device(): other = lax.ppermute(third[:, 0:2 * block], 'core', [(0, 1), (1, 0)])]
  transfers between devices with their start and end apart: 1 -> 2, of which waited for: 1 -> 2; matrix products, arithmetic and copies ran while one was open for 0% -> 0% of each run, Pallas kernels for 0% -> 0%
where the time goes in v3:
time: 92.3 us; the launch traced here: 91.8 us
  blocking collectives  55.2 us (60%)
  Pallas kernels  24.9 us (27%)
  starting transfers between devices  6.89 us (7%)
  waiting for transfers between devices  2.48 us (3%)
  local copies, waits for them, and re-layouts  1.48 us (2%)
    all_to_all x1, blocking collectives, on_device(): third = lax.all_to_all(sent, LAG, 0, 0, tiled=True)  23 us
    all_to_all x1, blocking collectives, on_device(): arrived = lax.all_to_all(pieces, LAG, 0, 0, tiled=True)  17.8 us
    all_to_all x1, blocking collectives, on_device(): gathered = lax.all_to_all(sent, 'zh', 0, 0, tiled=True)  14.3 us
    pallas_call x1, Pallas kernels, on_device(): pl.pallas_call(analyse_kernel, in_specs=[smem, away, away, vmem, vmem], o...  14.1 us
    pallas_call x1, Pallas kernels, on_device(): pl.pallas_call(observe_kernel, in_specs=[smem, vmem, vmem, away], out_spe...  6.81 us
    ppermute x1, starting transfers between devices, on_device(): swapped = lax.ppermute(gathered, 'core', [(0, 1), (1, 0)])  4.37 us
    ppermute x1, starting transfers between devices, on_device(): other = lax.ppermute(third[:, 0:2 * block], 'core', [(0, 1), (1, 0)])  2.52 us
    pallas_call x1, Pallas kernels, on_device(): pl.pallas_call(prepare_kernel, out_shape=[jax.ShapeDtypeStruct((members,...  2.33 us
  transfers between devices with their start and end apart: 2, of which 2 were waited for; matrix products, arithmetic and copies ran while one was open for 0% of the time, Pallas kernels for 0%

profile of v3, /device:TPU:1, one launch (start us, length us, event | category | flops | bytes accessed | tf_op | source)
XLA Modules:
  0.0 91.8 jit_solution(15473367392327604661)
XLA Ops:
  0.6 2.3 %prepare.1 = (bf16[1024,128]{1,0:T(8,128)(2,1)}, bf16[32,48,128]{2,1,0:T(8,128)(2,1)}, bf16[56,128]{1,0:T(8,128)(2,1)}) custom-call(bf16[1,128,1024]{2,1,0:T(8,128)(2,1)} %slab.1, s32[6,128]{1,0:T(8,128)} %shift.1, f32[6,128]{1,0:T(8,128)} %coupling.1, s32[2,4,16]{2,1,0:T(4,128)} %cells.1, f32[2,4,16]{2,1,0:T(4,128)} %weight.1, f32[2,16]{1,0:T(2,128)} %reading.1, ...), custom_call_target="tpu_custom_call" | custom-call | tf_op jit(solution)/shard_map/prepare/pallas_call | solution.py:497
  3.0 17.8 %all_to_all.15.arrived = bf16[32,48,128]{2,1,0:T(8,128)(2,1)} all-to-all(bf16[32,48,128]{2,1,0:T(8,128)(2,1)} %get-tuple-element.5), channel_id=1, replica_groups=mesh['lag_0'=4,'lag_1'=2,'lag_2'=4,'zh'=4,'core'=2] {'lag_0','lag_1','la..., dimensions={0} | all-to-all | bytes 786432 | tf_op jit(solution)/shard_map/all_to_all | solution.py:508
  20.8 1.7 %select.1 = bf16[4,96,128]{2,1,0:T(8,128)(2,1)} custom-call(s32[32]{0:T(128)} %order.5, bf16[32,48,128]{2,1,0:T(8,128)(2,1)} %all_to_all.15.arrived, bf16[56,128]{1,0:T(8,128)(2,1)} %get-tuple-element.6.extra), custom_call_target="tpu_custom_call" | custom-call | tf_op jit(solution)/shard_map/select/pallas_call | solution.py:513
  22.5 14.3 %all_to_all.16.one = bf16[4,96,128]{2,1,0:T(8,128)(2,1)S(1)} all-to-all(bf16[4,96,128]{2,1,0:T(8,128)(2,1)} %select.1), channel_id=1, replica_groups=mesh['lag_0'=4,'lag_1'=2,'lag_2'=4,'zh'=4,'core'=2] {'zh'}, dimensions={0} | all-to-all | bytes 196608 | tf_op jit(solution)/shard_map/all_to_all | solution.py:520
  36.8 0.0 copy-start.2
  36.8 4.4 %collective-permute-start = (bf16[4,96,128]{2,1,0:T(8,128)(2,1)S(1)}, bf16[4,96,128]{2,1,0:T(8,128)(2,1)S(1)}, u32[]{:S(2)}, u32[]{:S(2)}) collective-permute-start(bf16[4,96,128]{2,1,0:T(8,128)(2,1)S(1)} %all_to_all.16.one), channel_id=1, source_target_pairs={{0,1},{1,0},{2,3},{3,2},{4,5},{5,4},{6,7},{7,6},{8,9},{9,8},{10,11... | collective-permute-start | bytes 294920 | tf_op jit(solution)/shard_map/ppermute | solution.py:521
  41.2 0.9 %collective-permute-done.two = bf16[4,96,128]{2,1,0:T(8,128)(2,1)S(1)} collective-permute-done((bf16[4,96,128]{2,1,0:T(8,128)(2,1)S(1)}, bf16[4,96,128]{2,1,0:T(8,128)(2,1)S(1)}, u32[]{:S(2)}, u32[]{:S(2)}) %collective-permute-start) | collective-permute-done | bytes 98336 | tf_op jit(solution)/shard_map/ppermute | solution.py:521
  42.1 0.0 copy-done.2
  42.1 0.0 copy-start.3
  42.1 0.6 copy-done.3
  42.8 6.8 %observe.1 = bf16[32,160,128]{2,1,0:T(8,128)(2,1)} custom-call(s32[32]{0:T(128)} %order.5, bf16[4,96,128]{2,1,0:T(8,128)(2,1)} %copy-done.2, bf16[4,96,128]{2,1,0:T(8,128)(2,1)} %copy-done.3, bf16[32,48,128]{2,1,0:T(8,128)(2,1)} %all_to_all.15.arrived), custom_call_target="tpu_custom_call" | custom-call | tf_op jit(solution)/shard_map/observe/pallas_call | solution.py:524
  49.6 23.0 %all_to_all.17.got = bf16[32,160,128]{2,1,0:T(8,128)(2,1)S(1)} all-to-all(bf16[32,160,128]{2,1,0:T(8,128)(2,1)} %observe.1), channel_id=1, replica_groups=mesh['lag_0'=4,'lag_1'=2,'lag_2'=4,'zh'=4,'core'=2] {'lag_0','lag_1','la..., dimensions={0} | all-to-all | bytes 2621440 | tf_op jit(solution)/shard_map/all_to_all | solution.py:541
  72.6 0.0 copy-start
  72.7 2.5 %collective-permute-start.1 = (bf16[32,64,128]{2,1,0:T(8,128)(2,1)S(1)}, bf16[32,64,128]{2,1,0:T(8,128)(2,1)S(1)}, u32[]{:S(2)}, u32[]{:S(2)}) collective-permute-start(bf16[32,64,128]{2,1,0:T(8,128)(2,1)S(1)} %slice.4), channel_id=1, source_target_pairs={{0,1},{1,0},{2,3},{3,2},{4,5},{5,4},{6,7},{7,6},{8,9},{9,8},{10,11... | collective-permute-start | bytes 1572872 | tf_op jit(solution)/shard_map/ppermute | solution.py:542
  75.2 1.5 %collective-permute-done.1.other = bf16[32,64,128]{2,1,0:T(8,128)(2,1)S(1)} collective-permute-done((bf16[32,64,128]{2,1,0:T(8,128)(2,1)S(1)}, bf16[32,64,128]{2,1,0:T(8,128)(2,1)S(1)}, u32[]{:S(2)}, u32[]{:S(2)}) %collective-permute-start.1) | collective-permute-done | bytes 524320 | tf_op jit(solution)/shard_map/ppermute | solution.py:542
  76.7 0.0 copy-start.1
  76.7 0.0 copy-done
  76.7 0.8 copy-done.1
  77.5 14.1 %analyse.1 = (bf16[1,128,1024]{2,1,0:T(8,128)(2,1)}, bf16[2,32,128]{2,1,0:T(8,128)(2,1)}) custom-call(s32[32]{0:T(128)} %order.5, bf16[32,160,128]{2,1,0:T(8,128)(2,1)} %copy-done, bf16[32,64,128]{2,1,0:T(8,128)(2,1)} %copy-done.1, bf16[1024,128]{1,0:T(8,128)(2,1)} %get-tuple-element.7.slab_t, f32[2,128]{1,0:T(2,128)} %variance.3), custom_call_target="tpu_custom_call" | custom-call | tf_op jit(solution)/shard_map/analyse/pallas_call | solution.py:545
  (1 shorter events, 0.0 us)
Async XLA Ops:
  36.8 5.3 %copy-start.2 = (bf16[4,96,128]{2,1,0:T(8,128)(2,1)}, bf16[4,96,128]{2,1,0:T(8,128)(2,1)S(1)}, u32[]{:S(2)}) copy-start(bf16[4,96,128]{2,1,0:T(8,128)(2,1)S(1)} %all_to_all.16.one) | copy-start | bytes 294916
  36.8 5.3 %collective-permute-start = (bf16[4,96,128]{2,1,0:T(8,128)(2,1)S(1)}, bf16[4,96,128]{2,1,0:T(8,128)(2,1)S(1)}, u32[]{:S(2)}, u32[]{:S(2)}) collective-permute-start(bf16[4,96,128]{2,1,0:T(8,128)(2,1)S(1)} %all_to_all.16.one), channel_id=1, source_target_pairs={{0,1},{1,0},{2,3},{3,2},{4,5},{5,4},{6,7},{7,6},{8,9},{9,8},{10,11... | collective-permute-start | bytes 294920 | tf_op jit(solution)/shard_map/ppermute | solution.py:521
  42.1 0.6 copy-start.3
  72.6 4.1 %copy-start = (bf16[32,160,128]{2,1,0:T(8,128)(2,1)}, bf16[32,160,128]{2,1,0:T(8,128)(2,1)S(1)}, u32[]{:S(2)}) copy-start(bf16[32,160,128]{2,1,0:T(8,128)(2,1)S(1)} %all_to_all.17.got) | copy-start | bytes 3932164
  72.7 4.1 %collective-permute-start.1 = (bf16[32,64,128]{2,1,0:T(8,128)(2,1)S(1)}, bf16[32,64,128]{2,1,0:T(8,128)(2,1)S(1)}, u32[]{:S(2)}, u32[]{:S(2)}) collective-permute-start(bf16[32,64,128]{2,1,0:T(8,128)(2,1)S(1)} %slice.4), channel_id=1, source_target_pairs={{0,1},{1,0},{2,3},{3,2},{4,5},{5,4},{6,7},{7,6},{8,9},{9,8},{10,11... | collective-permute-start | bytes 1572872 | tf_op jit(solution)/shard_map/ppermute | solution.py:542
  76.7 0.8 copy-start.1

commit v4 on v3

--- a/solution.py
+++ b/solution.py
@@ -14,7 +14,7 @@
 LANES = 128
 FIRST_ROWS = 48
 SECOND_ROWS = 96
-THIRD = 5
+THIRD = 4
 
 
 def split3(x):
@@ -171,14 +171,17 @@
     return total
 
 
-def observe_kernel(order, one, two, arrived, out, got, state, fields, matrix, total, common, own, sems):
+def observe_kernel(order, one, two, arrived, out, got, state, fields, matrix, total, piece, sems):
     blocks = got.shape[0]
     lags = out.shape[0]
+    firsts = (order[lags - 1], order[lags - 2])
     fetch = [
         pltpu.make_async_copy(
-            arrived.at[order[lags - 1 - i], pl.ds(0, 32), :], common.at[pl.ds(64 + 32 * i, 32), :], sems.at[2, i]
+            arrived.at[firsts[i], pl.ds(0, 32), :], piece.at[v, pl.ds(64 + 32 * i, 32), :], sems.at[1, 3 * i + v]
         )
         for i in range(2)
+        for v in range(3)
+        if v != i + 1
     ]
     for copy in fetch:
         copy.start()
@@ -189,9 +192,9 @@
         got[2 * z + 1 - core] = two[z]
     build_mesh(got, matrix, total)
     for b in range(blocks):
-        piece = got[b, 0:48, :].astype(F32)
-        mean = piece[32:33] + piece[33:34] + piece[34:35]
-        state[b] = jnp.concatenate([piece[0:32], jnp.broadcast_to(mean, (8, LANES))], axis=0)
+        block = got[b, 0:48, :].astype(F32)
+        mean = block[32:33] + block[33:34] + block[34:35]
+        state[b] = jnp.concatenate([block[0:32], jnp.broadcast_to(mean, (8, LANES))], axis=0)
     relax(matrix, total, state)
     forecast = []
     for b in range(blocks):
@@ -201,25 +204,26 @@
         value = jnp.concatenate([rounded.astype(F32), value[32:40]], axis=0)
         state[b] = value
         forecast.append(value)
-    own[0] = fields[space_rank]
+    piece[1, 64:96, :] = fields[space_rank]
     error, cells, weight = observation_rows(got, 0)
     seen = measure(forecast, cells, weight)
     spread = seen[0:32] - seen[32:33]
     innovation = error - seen[0:32]
     relax(matrix, total, state)
-    own[1] = to_bf16(state[space_rank, 0:32, :])
+    piece[2, 96:128, :] = to_bf16(state[space_rank, 0:32, :])
     error, cells, weight = observation_rows(got, 1)
     seen = measure([state[b] for b in range(blocks)], cells, weight)
-    common[0:32] = to_bf16(jnp.where(core == 0, spread, seen[0:32] - seen[32:33]))
-    common[32:64] = to_bf16(jnp.where(core == 0, innovation, error - seen[0:32]))
+    spread = to_bf16(jnp.where(core == 0, spread, seen[0:32] - seen[32:33]))
+    innovation = to_bf16(jnp.where(core == 0, innovation, error - seen[0:32]))
+    for v in range(3):
+        piece[v, 0:32, :] = spread
+        piece[v, 32:64, :] = innovation
     for copy in fetch:
         copy.wait()
-    second = order[lags - 2]
     copies = []
     for r in range(lags):
-        pick = jnp.where(second == r, 1, 0)
-        copies.append(pltpu.make_async_copy(common, out.at[r, pl.ds(0, 128), :], sems.at[0, r]))
-        copies.append(pltpu.make_async_copy(own.at[pick], out.at[r, pl.ds(128, 32), :], sems.at[1, r]))
+        pick = jnp.where(firsts[0] == r, 1, jnp.where(firsts[1] == r, 2, 0))
+        copies.append(pltpu.make_async_copy(piece.at[pick], out.at[r], sems.at[0, r]))
     for copy in copies:
         copy.start()
     for copy in copies:
@@ -355,7 +359,7 @@
 
 
 def analyse_kernel(
-    order, got, other, slab_t, variance, analysed, retired, parts, now, cent, gain, left, right, solved, sems
+    order, got, other, slab_t, variance, analysed, retired, now, cent, gain, left, right, solved
 ):
     lags = got.shape[0]
     lag_rank, _ = ranks()
@@ -364,28 +368,13 @@
     mine = pl.ds(pl.multiple_of(lag_rank * block, block), block)
     own_core = lax.axis_index("core")
 
-    def copy_of(source, i, to):
-        return pltpu.make_async_copy(source.at[:, pl.ds(block * i, block), :], parts.at[to], sems.at[to])
-
-    for i in range(2):
-        for core in range(2):
-
-            @pl.when(own_core == core)
-            def _():
-                copy_of(got, i, 2 * core + i).start()
-                copy_of(other, i, 2 * (1 - core) + i).start()
-
-    for i in range(3):
-        copy_of(got, 2 + i, 4 + i).start()
-
-    def wait(i):
-        copy_of(got, 0, i).wait()
-
     def part(i):
-        return parts[i].reshape(members, LANES)
+        rows = slice(i % 2 * block, (i % 2 + 1) * block)
+        values = jnp.where(own_core == i // 2, got[:, rows, :], other[:, rows, :])
+        return values.reshape(members, LANES)
 
     chunks = [slice(LANES * c, LANES * c + LANES) for c in range(members // LANES)]
-    took = (lag_rank == order[lags - 1]) | (lag_rank == order[lags - 2])
+    holds = (lag_rank == order[lags - 1], lag_rank == order[lags - 2])
 
     def folded(values):
         return values.reshape(values.shape[0] // 8, 8, LANES).sum(axis=0)
@@ -414,11 +403,8 @@
     def gain_job(i, spread, values):
         return lambda: put_gain(gain, i, spread, values())
 
-    wait(0)
     spread = turned(part(0))
     gram = gram_of(spread, part(0), variance[0:1, :])
-    for i in range(1, 7):
-        wait(i)
 
     def keep(i, load):
         def loaded(rows):
@@ -429,14 +415,20 @@
         return loaded
 
     def rows_of(i, rows):
-        return parts[i, rows.start // block : rows.stop // block].reshape(LANES, LANES)
+        return got[rows.start // block : rows.stop // block, i * block : (i + 1) * block, :].reshape(LANES, LANES)
+
+    def own_rows(rows):
+        return jnp.where(holds[0], rows_of(2, rows), jnp.where(holds[1], rows_of(3, rows), slab_t[rows, :]))
+
+    def retiring(i):
+        return lambda rows: jnp.where(holds[i], slab_t[rows, :], rows_of(2 + i, rows))
 
     jobs = [gain_job(3, spread, lambda: part(2))]
-    jobs += centre_jobs(0, keep(0, lambda rows: jnp.where(took, rows_of(6, rows), slab_t[rows, :])))
+    jobs += centre_jobs(0, keep(0, own_rows))
     jobs += [gain_job(0, spread, lambda: cent[0])]
-    jobs += centre_jobs(1, keep(1, lambda rows: rows_of(5, rows)))
+    jobs += centre_jobs(1, keep(1, retiring(1)))
     jobs += [gain_job(1, spread, lambda: cent[1])]
-    jobs += centre_jobs(2, keep(2, lambda rows: rows_of(4, rows)))
+    jobs += centre_jobs(2, keep(2, retiring(0)))
     jobs += [gain_job(2, spread, lambda: cent[2])]
     solved[...] = doubled(to_bf16(dot(doubled(part(1)), stacked(inverse(gram, left, right, jobs)))))
     seen = change(gain, 3, solved[...])
@@ -464,8 +456,8 @@
     retired[1] = to_bf16(now[1, mine, :].astype(F32) + change(gain, 1, solved[mine, :]))
 
 
-def whole(shape):
-    return pl.BlockSpec(shape, lambda i, *_: (0,) * len(shape))
+def stay(values):
+    return pltpu.with_memory_space_constraint(values, pltpu.VMEM)
 
 
 def on_device(
@@ -519,6 +511,7 @@
     )(slot_order, arrived, extra)
     gathered = lax.all_to_all(sent, "zh", 0, 0, tiled=True)
     swapped = lax.ppermute(gathered, "core", [(0, 1), (1, 0)])
+    gathered, swapped = stay(gathered), stay(swapped)
 
     block = members // lags
     sent = pl.pallas_call(
@@ -532,33 +525,31 @@
             pltpu.VMEM((spaces, block, LANES), BF16),
             pltpu.VMEM((2, spaces, 2 * LANES, LANES), BF16),
             pltpu.VMEM((spaces, 8, LANES), F32),
-            pltpu.VMEM(((THIRD - 1) * block, LANES), BF16),
-            pltpu.VMEM((2, block, LANES), BF16),
-            pltpu.SemaphoreType.DMA((3, lags)),
+            pltpu.VMEM((3, THIRD * block, LANES), BF16),
+            pltpu.SemaphoreType.DMA((2, lags)),
         ],
         name="observe",
     )(slot_order, gathered, swapped, arrived)
     third = lax.all_to_all(sent, LAG, 0, 0, tiled=True)
     other = lax.ppermute(third[:, 0 : 2 * block], "core", [(0, 1), (1, 0)])
+    third, other = stay(third), stay(other)
 
     square = pltpu.VMEM((LANES, LANES), F32)
     return pl.pallas_call(
         analyse_kernel,
-        in_specs=[smem, away, away, vmem, vmem],
+        in_specs=[smem, vmem, vmem, vmem, vmem],
         out_specs=[vmem, vmem],
         out_shape=[
             jax.ShapeDtypeStruct(ensemble.shape, BF16),
             jax.ShapeDtypeStruct((CYCLES, block, LANES), BF16),
         ],
         scratch_shapes=[
-            pltpu.VMEM((THIRD + 2, lags, block, LANES), BF16),
             pltpu.VMEM((3, members, LANES), BF16),
             pltpu.VMEM((3, members, LANES), BF16),
             pltpu.VMEM((4, 2 * LANES, LANES), BF16),
             square,
             square,
             pltpu.VMEM((members, 2 * LANES), BF16),
-            pltpu.SemaphoreType.DMA((THIRD + 2,)),
         ],
         name="analyse",
     )(slot_order, third, other, slab_t, observation_variance)

time: 92.3 us -> 85 us (0.921)
  blocking collectives: 55.2 us -> 52 us
  Pallas kernels: 24.9 us -> 23.3 us
  local copies, waits for them, and re-layouts: 1.48 us -> 0.04 us
    all_to_all x1, blocking collectives: 23 us -> 19.8 us  [on_device(): third = lax.all_to_all(sent, LAG, 0, 0, tiled=True)]
    unnamed x8 -> x0, local copies, waits for them, and re-layouts: 1.43 us -> none
where the time goes in v4:
time: 85 us; the launch traced here: 84.5 us
  blocking collectives  52 us (61%)
  Pallas kernels  23.3 us (27%)
  starting transfers between devices  6.11 us (7%)
  waiting for transfers between devices  2.48 us (3%)
    all_to_all x1, blocking collectives, on_device(): third = lax.all_to_all(sent, LAG, 0, 0, tiled=True)  19.8 us
    all_to_all x1, blocking collectives, on_device(): arrived = lax.all_to_all(pieces, LAG, 0, 0, tiled=True)  17.8 us
    all_to_all x1, blocking collectives, on_device(): gathered = lax.all_to_all(sent, 'zh', 0, 0, tiled=True)  14.3 us
    pallas_call x1, Pallas kernels, on_device(): pl.pallas_call(analyse_kernel, in_specs=[smem, vmem, vmem, vmem, vmem], o...  13.2 us
    pallas_call x1, Pallas kernels, on_device(): pl.pallas_call(observe_kernel, in_specs=[smem, vmem, vmem, away], out_spe...  6.13 us
    ppermute x1, starting transfers between devices, on_device(): swapped = lax.ppermute(gathered, 'core', [(0, 1), (1, 0)])  4.37 us
    pallas_call x1, Pallas kernels, on_device(): pl.pallas_call(prepare_kernel, out_shape=[jax.ShapeDtypeStruct((members,...  2.32 us
    ppermute x1, starting transfers between devices, on_device(): other = lax.ppermute(third[:, 0:2 * block], 'core', [(0, 1), (1, 0)])  1.73 us
  transfers between devices with their start and end apart: 2, of which 2 were waited for; matrix products, arithmetic and copies ran while one was open for 0% of the time, Pallas kernels for 0%

profile of v4, /device:TPU:1, one launch (start us, length us, event | category | flops | bytes accessed | tf_op | source)
XLA Modules:
  0.0 84.5 jit_solution(11492378074551967955)
XLA Ops:
  0.6 2.3 %prepare.1 = (bf16[1024,128]{1,0:T(8,128)(2,1)}, bf16[32,48,128]{2,1,0:T(8,128)(2,1)}, bf16[56,128]{1,0:T(8,128)(2,1)}) custom-call(bf16[1,128,1024]{2,1,0:T(8,128)(2,1)} %slab.1, s32[6,128]{1,0:T(8,128)} %shift.1, f32[6,128]{1,0:T(8,128)} %coupling.1, s32[2,4,16]{2,1,0:T(4,128)} %cells.1, f32[2,4,16]{2,1,0:T(4,128)} %weight.1, f32[2,16]{1,0:T(2,128)} %reading.1, ...), custom_call_target="tpu_custom_call" | custom-call | tf_op jit(solution)/shard_map/prepare/pallas_call | solution.py:489
  2.9 17.8 %all_to_all.15.arrived = bf16[32,48,128]{2,1,0:T(8,128)(2,1)} all-to-all(bf16[32,48,128]{2,1,0:T(8,128)(2,1)} %get-tuple-element.5), channel_id=1, replica_groups=mesh['lag_0'=4,'lag_1'=2,'lag_2'=4,'zh'=4,'core'=2] {'lag_0','lag_1','la..., dimensions={0} | all-to-all | bytes 786432 | tf_op jit(solution)/shard_map/all_to_all | solution.py:500
  20.8 1.7 %select.1 = bf16[4,96,128]{2,1,0:T(8,128)(2,1)} custom-call(s32[32]{0:T(128)} %order.5, bf16[32,48,128]{2,1,0:T(8,128)(2,1)} %all_to_all.15.arrived, bf16[56,128]{1,0:T(8,128)(2,1)} %get-tuple-element.6.extra), custom_call_target="tpu_custom_call" | custom-call | tf_op jit(solution)/shard_map/select/pallas_call | solution.py:505
  22.5 14.3 %all_to_all.16.one = bf16[4,96,128]{2,1,0:T(8,128)(2,1)S(1)} all-to-all(bf16[4,96,128]{2,1,0:T(8,128)(2,1)} %select.1), channel_id=1, replica_groups=mesh['lag_0'=4,'lag_1'=2,'lag_2'=4,'zh'=4,'core'=2] {'zh'}, dimensions={0} | all-to-all | bytes 196608 | tf_op jit(solution)/shard_map/all_to_all | solution.py:512
  36.8 4.4 %collective-permute-start = (bf16[4,96,128]{2,1,0:T(8,128)(2,1)S(1)}, bf16[4,96,128]{2,1,0:T(8,128)(2,1)S(1)}, u32[]{:S(2)}, u32[]{:S(2)}) collective-permute-start(bf16[4,96,128]{2,1,0:T(8,128)(2,1)S(1)} %all_to_all.16.one), channel_id=1, source_target_pairs={{0,1},{1,0},{2,3},{3,2},{4,5},{5,4},{6,7},{7,6},{8,9},{9,8},{10,11... | collective-permute-start | bytes 294920 | tf_op jit(solution)/shard_map/ppermute | solution.py:513
  41.2 0.9 %collective-permute-done.two = bf16[4,96,128]{2,1,0:T(8,128)(2,1)S(1)} collective-permute-done((bf16[4,96,128]{2,1,0:T(8,128)(2,1)S(1)}, bf16[4,96,128]{2,1,0:T(8,128)(2,1)S(1)}, u32[]{:S(2)}, u32[]{:S(2)}) %collective-permute-start) | collective-permute-done | bytes 98336 | tf_op jit(solution)/shard_map/ppermute | solution.py:513
  42.1 6.1 %observe.1 = bf16[32,128,128]{2,1,0:T(8,128)(2,1)} custom-call(s32[32]{0:T(128)} %order.5, bf16[4,96,128]{2,1,0:T(8,128)(2,1)S(1)} %all_to_all.16.one, bf16[4,96,128]{2,1,0:T(8,128)(2,1)S(1)} %collective-permute-done.two, bf16[32,48,128]{2,1,0:T(8,128)(2,1)} %all_to_all.15.arrived), custom_call_target="tpu_custom_call" | custom-call | tf_op jit(solution)/shard_map/observe/pallas_call | solution.py:517
  48.3 19.8 %all_to_all.17.got = bf16[32,128,128]{2,1,0:T(8,128)(2,1)S(1)} all-to-all(bf16[32,128,128]{2,1,0:T(8,128)(2,1)} %observe.1), channel_id=1, replica_groups=mesh['lag_0'=4,'lag_1'=2,'lag_2'=4,'zh'=4,'core'=2] {'lag_0','lag_1','la..., dimensions={0} | all-to-all | bytes 2097152 | tf_op jit(solution)/shard_map/all_to_all | solution.py:533
  68.1 1.7 %collective-permute-start.1 = (bf16[32,64,128]{2,1,0:T(8,128)(2,1)S(1)}, bf16[32,64,128]{2,1,0:T(8,128)(2,1)S(1)}, u32[]{:S(2)}, u32[]{:S(2)}) collective-permute-start(bf16[32,64,128]{2,1,0:T(8,128)(2,1)S(1)} %slice.4), channel_id=1, source_target_pairs={{0,1},{1,0},{2,3},{3,2},{4,5},{5,4},{6,7},{7,6},{8,9},{9,8},{10,11... | collective-permute-start | bytes 1572872 | tf_op jit(solution)/shard_map/ppermute | solution.py:534
  69.8 1.5 %collective-permute-done.1.other = bf16[32,64,128]{2,1,0:T(8,128)(2,1)S(1)} collective-permute-done((bf16[32,64,128]{2,1,0:T(8,128)(2,1)S(1)}, bf16[32,64,128]{2,1,0:T(8,128)(2,1)S(1)}, u32[]{:S(2)}, u32[]{:S(2)}) %collective-permute-start.1) | collective-permute-done | bytes 524320 | tf_op jit(solution)/shard_map/ppermute | solution.py:534
  71.3 13.2 %analyse.1 = (bf16[1,128,1024]{2,1,0:T(8,128)(2,1)}, bf16[2,32,128]{2,1,0:T(8,128)(2,1)}) custom-call(s32[32]{0:T(128)} %order.5, bf16[32,128,128]{2,1,0:T(8,128)(2,1)S(1)} %all_to_all.17.got, bf16[32,64,128]{2,1,0:T(8,128)(2,1)S(1)} %collective-permute-done.1.other, bf16[1024,128]{1,0:T(8,128)(2,1)} %get-tuple-element.7.slab_t, f32[2,128]{1,0:T(2,128)} %variance.3), custom_call_target="tpu_custom_call" | custom-call | tf_op jit(solution)/shard_map/analyse/pallas_call | solution.py:538
  (1 shorter events, 0.0 us)
Async XLA Ops:
  36.8 5.3 %collective-permute-start = (bf16[4,96,128]{2,1,0:T(8,128)(2,1)S(1)}, bf16[4,96,128]{2,1,0:T(8,128)(2,1)S(1)}, u32[]{:S(2)}, u32[]{:S(2)}) collective-permute-start(bf16[4,96,128]{2,1,0:T(8,128)(2,1)S(1)} %all_to_all.16.one), channel_id=1, source_target_pairs={{0,1},{1,0},{2,3},{3,2},{4,5},{5,4},{6,7},{7,6},{8,9},{9,8},{10,11... | collective-permute-start | bytes 294920 | tf_op jit(solution)/shard_map/ppermute | solution.py:513
  68.1 3.3 %collective-permute-start.1 = (bf16[32,64,128]{2,1,0:T(8,128)(2,1)S(1)}, bf16[32,64,128]{2,1,0:T(8,128)(2,1)S(1)}, u32[]{:S(2)}, u32[]{:S(2)}) collective-permute-start(bf16[32,64,128]{2,1,0:T(8,128)(2,1)S(1)} %slice.4), channel_id=1, source_target_pairs={{0,1},{1,0},{2,3},{3,2},{4,5},{5,4},{6,7},{7,6},{8,9},{9,8},{10,11... | collective-permute-start | bytes 1572872 | tf_op jit(solution)/shard_map/ppermute | solution.py:534

commit v5 on v4

--- a/solution.py
+++ b/solution.py
@@ -37,13 +37,12 @@
 ):
     values = slab[0].astype(F32)
     mean = jnp.mean(values, axis=1, keepdims=True)
-    turned = values.T
     mean_row = jnp.broadcast_to(mean, (LANES, LANES)).T[0:8]
     hi, mid, low = split3(mean_row)
     row8 = lax.broadcasted_iota(jnp.int32, (8, LANES), 0)
     tail = jnp.where(row8 == 0, hi, jnp.where(row8 == 1, mid, jnp.where(row8 == 2, low, 0.0)))
     tail = to_bf16(jnp.concatenate([tail, jnp.zeros((8, LANES), F32)], axis=0))
-    turned = to_bf16(turned)
+    turned = slab[0].T
     slab_t[...] = turned
     for r in range(32):
         pieces[r, 0:32, :] = turned[32 * r : 32 * r + 32]
@@ -175,16 +174,11 @@
     blocks = got.shape[0]
     lags = out.shape[0]
     firsts = (order[lags - 1], order[lags - 2])
-    fetch = [
-        pltpu.make_async_copy(
-            arrived.at[firsts[i], pl.ds(0, 32), :], piece.at[v, pl.ds(64 + 32 * i, 32), :], sems.at[1, 3 * i + v]
-        )
-        for i in range(2)
-        for v in range(3)
-        if v != i + 1
-    ]
-    for copy in fetch:
-        copy.start()
+    for i in range(2):
+        slab = arrived[firsts[i], 0:32, :]
+        for v in range(3):
+            if v != i + 1:
+                piece[v, 64 + 32 * i : 96 + 32 * i, :] = slab
     _, space_rank = ranks()
     core = lax.axis_index("core")
     for z in range(one.shape[0]):
@@ -218,12 +212,10 @@
     for v in range(3):
         piece[v, 0:32, :] = spread
         piece[v, 32:64, :] = innovation
-    for copy in fetch:
-        copy.wait()
     copies = []
     for r in range(lags):
         pick = jnp.where(firsts[0] == r, 1, jnp.where(firsts[1] == r, 2, 0))
-        copies.append(pltpu.make_async_copy(piece.at[pick], out.at[r], sems.at[0, r]))
+        copies.append(pltpu.make_async_copy(piece.at[pick], out.at[r], sems.at[r]))
     for copy in copies:
         copy.start()
     for copy in copies:
@@ -342,7 +334,7 @@
 
 
 def turned(values):
-    return values.astype(F32).T.astype(BF16)
+    return values.T
 
 
 def gram_of(spread, spread_t, variance):
@@ -451,7 +443,7 @@
     jobs = centre_jobs(0, renewed(0)) + centre_jobs(1, renewed(1)) + [retire_first]
     jobs += [gain_job(0, spread, lambda: cent[0]), gain_job(1, spread, lambda: cent[1])]
     solved_again = doubled(to_bf16(dot(doubled(innovation), stacked(inverse(gram, left, right, jobs)))))
-    analysed[0] = to_bf16((now[0].astype(F32) + change(gain, 0, solved_again)).T)
+    analysed[0] = to_bf16(now[0].astype(F32) + change(gain, 0, solved_again)).T
     solved[...] = solved_again
     retired[1] = to_bf16(now[1, mine, :].astype(F32) + change(gain, 1, solved[mine, :]))
 
@@ -497,7 +489,8 @@
         name="prepare",
     )(*inputs)
 
-    arrived = lax.all_to_all(pieces, LAG, 0, 0, tiled=True)
+    arrived = stay(lax.all_to_all(pieces, LAG, 0, 0, tiled=True))
+    slab_t, extra = stay(slab_t), stay(extra)
 
     vmem = pl.BlockSpec(memory_space=pltpu.VMEM)
     smem = pl.BlockSpec(memory_space=pltpu.SMEM)
@@ -516,7 +509,7 @@
     block = members // lags
     sent = pl.pallas_call(
         observe_kernel,
-        in_specs=[smem, vmem, vmem, away],
+        in_specs=[smem, vmem, vmem, vmem],
         out_specs=away,
         out_shape=jax.ShapeDtypeStruct((lags, THIRD * block, LANES), BF16),
         scratch_shapes=[
@@ -526,7 +519,7 @@
             pltpu.VMEM((2, spaces, 2 * LANES, LANES), BF16),
             pltpu.VMEM((spaces, 8, LANES), F32),
             pltpu.VMEM((3, THIRD * block, LANES), BF16),
-            pltpu.SemaphoreType.DMA((2, lags)),
+            pltpu.SemaphoreType.DMA((lags,)),
         ],
         name="observe",
     )(slot_order, gathered, swapped, arrived)

time: 85 us -> 83.8 us (0.986)
  Pallas kernels: 23.3 us -> 22.1 us
where the time goes in v5:
time: 83.8 us; the launch traced here: 83.3 us
  blocking collectives  52 us (62%)
  Pallas kernels  22.1 us (26%)
  starting transfers between devices  6.11 us (7%)
  waiting for transfers between devices  2.48 us (3%)
    all_to_all x1, blocking collectives, on_device(): third = lax.all_to_all(sent, LAG, 0, 0, tiled=True)  19.8 us
    all_to_all x1, blocking collectives, on_device(): arrived = stay(lax.all_to_all(pieces, LAG, 0, 0, tiled=True))  17.9 us
    all_to_all x1, blocking collectives, on_device(): gathered = lax.all_to_all(sent, 'zh', 0, 0, tiled=True)  14.3 us
    pallas_call x1, Pallas kernels, on_device(): pl.pallas_call(analyse_kernel, in_specs=[smem, vmem, vmem, vmem, vmem], o...  12.7 us
    pallas_call x1, Pallas kernels, on_device(): pl.pallas_call(observe_kernel, in_specs=[smem, vmem, vmem, vmem], out_spe...  5.84 us
    ppermute x1, starting transfers between devices, on_device(): swapped = lax.ppermute(gathered, 'core', [(0, 1), (1, 0)])  4.37 us
    pallas_call x1, Pallas kernels, on_device(): pl.pallas_call(prepare_kernel, out_shape=[jax.ShapeDtypeStruct((members,...  2.25 us
    ppermute x1, starting transfers between devices, on_device(): other = lax.ppermute(third[:, 0:2 * block], 'core', [(0, 1), (1, 0)])  1.74 us
  transfers between devices with their start and end apart: 2, of which 2 were waited for; matrix products, arithmetic and copies ran while one was open for 0% of the time, Pallas kernels for 0%

profile of v5, /device:TPU:1, one launch (start us, length us, event | category | flops | bytes accessed | tf_op | source)
XLA Modules:
  0.0 83.3 jit_solution(14814927380221345246)
XLA Ops:
  0.6 2.2 %prepare.1 = (bf16[1024,128]{1,0:T(8,128)(2,1)}, bf16[32,48,128]{2,1,0:T(8,128)(2,1)}, bf16[56,128]{1,0:T(8,128)(2,1)}) custom-call(bf16[1,128,1024]{2,1,0:T(8,128)(2,1)} %slab.1, s32[6,128]{1,0:T(8,128)} %shift.1, f32[6,128]{1,0:T(8,128)} %coupling.1, s32[2,4,16]{2,1,0:T(4,128)} %cells.1, f32[2,4,16]{2,1,0:T(4,128)} %weight.1, f32[2,16]{1,0:T(2,128)} %reading.1, ...), custom_call_target="tpu_custom_call" | custom-call | tf_op jit(solution)/shard_map/prepare/pallas_call | solution.py:481
  2.9 0.0 copy-start.1
  2.9 17.9 %all_to_all.15.arrived = bf16[32,48,128]{2,1,0:T(8,128)(2,1)S(1)} all-to-all(bf16[32,48,128]{2,1,0:T(8,128)(2,1)} %get-tuple-element.5), channel_id=1, replica_groups=mesh['lag_0'=4,'lag_1'=2,'lag_2'=4,'zh'=4,'core'=2] {'lag_0','lag_1','la..., dimensions={0} | all-to-all | bytes 786432 | tf_op jit(solution)/shard_map/all_to_all | solution.py:492
  20.8 0.0 copy-done.1
  20.8 1.3 %select.1 = bf16[4,96,128]{2,1,0:T(8,128)(2,1)} custom-call(s32[32]{0:T(128)} %order.5, bf16[32,48,128]{2,1,0:T(8,128)(2,1)S(1)} %all_to_all.15.arrived, bf16[56,128]{1,0:T(8,128)(2,1)S(1)} %copy-done.1), custom_call_target="tpu_custom_call" | custom-call | tf_op jit(solution)/shard_map/select/pallas_call | solution.py:498
  22.1 14.3 %all_to_all.16.one = bf16[4,96,128]{2,1,0:T(8,128)(2,1)S(1)} all-to-all(bf16[4,96,128]{2,1,0:T(8,128)(2,1)} %select.1), channel_id=1, replica_groups=mesh['lag_0'=4,'lag_1'=2,'lag_2'=4,'zh'=4,'core'=2] {'zh'}, dimensions={0} | all-to-all | bytes 196608 | tf_op jit(solution)/shard_map/all_to_all | solution.py:505
  36.4 4.4 %collective-permute-start = (bf16[4,96,128]{2,1,0:T(8,128)(2,1)S(1)}, bf16[4,96,128]{2,1,0:T(8,128)(2,1)S(1)}, u32[]{:S(2)}, u32[]{:S(2)}) collective-permute-start(bf16[4,96,128]{2,1,0:T(8,128)(2,1)S(1)} %all_to_all.16.one), channel_id=1, source_target_pairs={{0,1},{1,0},{2,3},{3,2},{4,5},{5,4},{6,7},{7,6},{8,9},{9,8},{10,11... | collective-permute-start | bytes 294920 | tf_op jit(solution)/shard_map/ppermute | solution.py:506
  40.8 0.9 %collective-permute-done.two = bf16[4,96,128]{2,1,0:T(8,128)(2,1)S(1)} collective-permute-done((bf16[4,96,128]{2,1,0:T(8,128)(2,1)S(1)}, bf16[4,96,128]{2,1,0:T(8,128)(2,1)S(1)}, u32[]{:S(2)}, u32[]{:S(2)}) %collective-permute-start) | collective-permute-done | bytes 98336 | tf_op jit(solution)/shard_map/ppermute | solution.py:506
  41.7 5.8 %observe.1 = bf16[32,128,128]{2,1,0:T(8,128)(2,1)} custom-call(s32[32]{0:T(128)} %order.5, bf16[4,96,128]{2,1,0:T(8,128)(2,1)S(1)} %all_to_all.16.one, bf16[4,96,128]{2,1,0:T(8,128)(2,1)S(1)} %collective-permute-done.two, bf16[32,48,128]{2,1,0:T(8,128)(2,1)S(1)} %all_to_all.15.arrived), custom_call_target="tpu_custom_call" | custom-call | tf_op jit(solution)/shard_map/observe/pallas_call | solution.py:510
  47.6 19.8 %all_to_all.17.got = bf16[32,128,128]{2,1,0:T(8,128)(2,1)S(1)} all-to-all(bf16[32,128,128]{2,1,0:T(8,128)(2,1)} %observe.1), channel_id=1, replica_groups=mesh['lag_0'=4,'lag_1'=2,'lag_2'=4,'zh'=4,'core'=2] {'lag_0','lag_1','la..., dimensions={0} | all-to-all | bytes 2097152 | tf_op jit(solution)/shard_map/all_to_all | solution.py:526
  67.3 0.0 copy-start
  67.4 1.7 %collective-permute-start.1 = (bf16[32,64,128]{2,1,0:T(8,128)(2,1)S(1)}, bf16[32,64,128]{2,1,0:T(8,128)(2,1)S(1)}, u32[]{:S(2)}, u32[]{:S(2)}) collective-permute-start(bf16[32,64,128]{2,1,0:T(8,128)(2,1)S(1)} %slice.4), channel_id=1, source_target_pairs={{0,1},{1,0},{2,3},{3,2},{4,5},{5,4},{6,7},{7,6},{8,9},{9,8},{10,11... | collective-permute-start | bytes 1572872 | tf_op jit(solution)/shard_map/ppermute | solution.py:527
  69.1 1.5 %collective-permute-done.1.other = bf16[32,64,128]{2,1,0:T(8,128)(2,1)S(1)} collective-permute-done((bf16[32,64,128]{2,1,0:T(8,128)(2,1)S(1)}, bf16[32,64,128]{2,1,0:T(8,128)(2,1)S(1)}, u32[]{:S(2)}, u32[]{:S(2)}) %collective-permute-start.1) | collective-permute-done | bytes 524320 | tf_op jit(solution)/shard_map/ppermute | solution.py:527
  70.7 0.0 copy-done
  70.7 12.7 %analyse.1 = (bf16[1,128,1024]{2,1,0:T(8,128)(2,1)}, bf16[2,32,128]{2,1,0:T(8,128)(2,1)}) custom-call(s32[32]{0:T(128)} %order.5, bf16[32,128,128]{2,1,0:T(8,128)(2,1)S(1)} %all_to_all.17.got, bf16[32,64,128]{2,1,0:T(8,128)(2,1)S(1)} %collective-permute-done.1.other, bf16[1024,128]{1,0:T(8,128)(2,1)S(1)} %copy-done, f32[2,128]{1,0:T(2,128)} %variance.3), custom_call_target="tpu_custom_call" | custom-call | tf_op jit(solution)/shard_map/analyse/pallas_call | solution.py:531
  (1 shorter events, 0.0 us)
Async XLA Ops:
  2.9 17.9 %copy-start.1 = (bf16[56,128]{1,0:T(8,128)(2,1)S(1)}, bf16[56,128]{1,0:T(8,128)(2,1)}, u32[]{:S(2)}) copy-start(bf16[56,128]{1,0:T(8,128)(2,1)} %get-tuple-element.6.extra) | copy-start | bytes 43012
  36.4 5.3 %collective-permute-start = (bf16[4,96,128]{2,1,0:T(8,128)(2,1)S(1)}, bf16[4,96,128]{2,1,0:T(8,128)(2,1)S(1)}, u32[]{:S(2)}, u32[]{:S(2)}) collective-permute-start(bf16[4,96,128]{2,1,0:T(8,128)(2,1)S(1)} %all_to_all.16.one), channel_id=1, source_target_pairs={{0,1},{1,0},{2,3},{3,2},{4,5},{5,4},{6,7},{7,6},{8,9},{9,8},{10,11... | collective-permute-start | bytes 294920 | tf_op jit(solution)/shard_map/ppermute | solution.py:506
  67.3 3.3 %copy-start = (bf16[1024,128]{1,0:T(8,128)(2,1)S(1)}, bf16[1024,128]{1,0:T(8,128)(2,1)}, u32[]{:S(2)}) copy-start(bf16[1024,128]{1,0:T(8,128)(2,1)} %get-tuple-element.7.slab_t) | copy-start | bytes 786436
  67.4 3.3 %collective-permute-start.1 = (bf16[32,64,128]{2,1,0:T(8,128)(2,1)S(1)}, bf16[32,64,128]{2,1,0:T(8,128)(2,1)S(1)}, u32[]{:S(2)}, u32[]{:S(2)}) collective-permute-start(bf16[32,64,128]{2,1,0:T(8,128)(2,1)S(1)} %slice.4), channel_id=1, source_target_pairs={{0,1},{1,0},{2,3},{3,2},{4,5},{5,4},{6,7},{7,6},{8,9},{9,8},{10,11... | collective-permute-start | bytes 1572872 | tf_op jit(solution)/shard_map/ppermute | solution.py:527

commit v6 on v5

--- a/solution.py
+++ b/solution.py
@@ -139,9 +139,10 @@
     blocks = state.shape[0]
     lane = lax.broadcasted_iota(jnp.int32, (40, LANES), 1)
 
-    def step(_, carry):
-        now = [state[b] for b in range(blocks)]
-        zero = jnp.zeros((40, LANES), F32)
+    zero = jnp.zeros((40, LANES), F32)
+    now = [state[b] for b in range(blocks)]
+    for _ in range(FC_STEPS):
+        after_step = []
         for b in range(blocks):
             before = now[b - 1] if b else zero
             after = now[b + 1] if b + 1 < blocks else zero
@@ -151,10 +152,10 @@
             wide = to_bf16(jnp.concatenate([hi, both - hi], axis=0))
             first = dot(wide, matrix[0, b])
             gain = first[0:40] + (first[40:80] + dot(wide[0:40], matrix[1, b]))
-            state[b] = now[b] + (gain - total[b, 0:1, :] * now[b])
-        return carry
-
-    lax.fori_loop(0, FC_STEPS, step, 0)
+            after_step.append(now[b] + (gain - total[b, 0:1, :] * now[b]))
+        now = after_step
+    for b in range(blocks):
+        state[b] = now[b]
 
 
 def measure(values, cells, weight):

time: 83.8 us -> 82.3 us (0.982)
  Pallas kernels: 22.1 us -> 20.5 us
    pallas_call x1, Pallas kernels: 5.84 us -> 4.32 us  [on_device(): pl.pallas_call(observe_kernel, in_specs=[smem, vmem, vmem, vmem], out_spe...]
where the time goes in v6:
time: 82.3 us; the launch traced here: 81.8 us
  blocking collectives  52 us (63%)
  Pallas kernels  20.5 us (25%)
  starting transfers between devices  6.11 us (7%)
  waiting for transfers between devices  2.48 us (3%)
    all_to_all x1, blocking collectives, on_device(): third = lax.all_to_all(sent, LAG, 0, 0, tiled=True)  19.8 us
    all_to_all x1, blocking collectives, on_device(): arrived = stay(lax.all_to_all(pieces, LAG, 0, 0, tiled=True))  17.9 us
    all_to_all x1, blocking collectives, on_device(): gathered = lax.all_to_all(sent, 'zh', 0, 0, tiled=True)  14.3 us
    pallas_call x1, Pallas kernels, on_device(): pl.pallas_call(analyse_kernel, in_specs=[smem, vmem, vmem, vmem, vmem], o...  12.7 us
    ppermute x1, starting transfers between devices, on_device(): swapped = lax.ppermute(gathered, 'core', [(0, 1), (1, 0)])  4.37 us
    pallas_call x1, Pallas kernels, on_device(): pl.pallas_call(observe_kernel, in_specs=[smem, vmem, vmem, vmem], out_spe...  4.32 us
    pallas_call x1, Pallas kernels, on_device(): pl.pallas_call(prepare_kernel, out_shape=[jax.ShapeDtypeStruct((members,...  2.25 us
    ppermute x1, starting transfers between devices, on_device(): other = lax.ppermute(third[:, 0:2 * block], 'core', [(0, 1), (1, 0)])  1.74 us
  transfers between devices with their start and end apart: 2, of which 2 were waited for; matrix products, arithmetic and copies ran while one was open for 0% of the time, Pallas kernels for 0%

profile of v6, /device:TPU:1, one launch (start us, length us, event | category | flops | bytes accessed | tf_op | source)
XLA Modules:
  0.0 81.8 jit_solution(17616489083431968443)
XLA Ops:
  0.6 2.2 %prepare.1 = (bf16[1024,128]{1,0:T(8,128)(2,1)}, bf16[32,48,128]{2,1,0:T(8,128)(2,1)}, bf16[56,128]{1,0:T(8,128)(2,1)}) custom-call(bf16[1,128,1024]{2,1,0:T(8,128)(2,1)} %slab.1, s32[6,128]{1,0:T(8,128)} %shift.1, f32[6,128]{1,0:T(8,128)} %coupling.1, s32[2,4,16]{2,1,0:T(4,128)} %cells.1, f32[2,4,16]{2,1,0:T(4,128)} %weight.1, f32[2,16]{1,0:T(2,128)} %reading.1, ...), custom_call_target="tpu_custom_call" | custom-call | tf_op jit(solution)/shard_map/prepare/pallas_call | solution.py:482
  2.9 0.0 copy-start.1
  2.9 17.9 %all_to_all.15.arrived = bf16[32,48,128]{2,1,0:T(8,128)(2,1)S(1)} all-to-all(bf16[32,48,128]{2,1,0:T(8,128)(2,1)} %get-tuple-element.5), channel_id=1, replica_groups=mesh['lag_0'=4,'lag_1'=2,'lag_2'=4,'zh'=4,'core'=2] {'lag_0','lag_1','la..., dimensions={0} | all-to-all | bytes 786432 | tf_op jit(solution)/shard_map/all_to_all | solution.py:493
  20.8 0.0 copy-done.1
  20.8 1.3 %select.1 = bf16[4,96,128]{2,1,0:T(8,128)(2,1)} custom-call(s32[32]{0:T(128)} %order.5, bf16[32,48,128]{2,1,0:T(8,128)(2,1)S(1)} %all_to_all.15.arrived, bf16[56,128]{1,0:T(8,128)(2,1)S(1)} %copy-done.1), custom_call_target="tpu_custom_call" | custom-call | tf_op jit(solution)/shard_map/select/pallas_call | solution.py:499
  22.1 14.3 %all_to_all.16.one = bf16[4,96,128]{2,1,0:T(8,128)(2,1)S(1)} all-to-all(bf16[4,96,128]{2,1,0:T(8,128)(2,1)} %select.1), channel_id=1, replica_groups=mesh['lag_0'=4,'lag_1'=2,'lag_2'=4,'zh'=4,'core'=2] {'zh'}, dimensions={0} | all-to-all | bytes 196608 | tf_op jit(solution)/shard_map/all_to_all | solution.py:506
  36.4 4.4 %collective-permute-start = (bf16[4,96,128]{2,1,0:T(8,128)(2,1)S(1)}, bf16[4,96,128]{2,1,0:T(8,128)(2,1)S(1)}, u32[]{:S(2)}, u32[]{:S(2)}) collective-permute-start(bf16[4,96,128]{2,1,0:T(8,128)(2,1)S(1)} %all_to_all.16.one), channel_id=1, source_target_pairs={{0,1},{1,0},{2,3},{3,2},{4,5},{5,4},{6,7},{7,6},{8,9},{9,8},{10,11... | collective-permute-start | bytes 294920 | tf_op jit(solution)/shard_map/ppermute | solution.py:507
  40.8 0.9 %collective-permute-done.two = bf16[4,96,128]{2,1,0:T(8,128)(2,1)S(1)} collective-permute-done((bf16[4,96,128]{2,1,0:T(8,128)(2,1)S(1)}, bf16[4,96,128]{2,1,0:T(8,128)(2,1)S(1)}, u32[]{:S(2)}, u32[]{:S(2)}) %collective-permute-start) | collective-permute-done | bytes 98336 | tf_op jit(solution)/shard_map/ppermute | solution.py:507
  41.7 4.3 %observe.1 = bf16[32,128,128]{2,1,0:T(8,128)(2,1)} custom-call(s32[32]{0:T(128)} %order.5, bf16[4,96,128]{2,1,0:T(8,128)(2,1)S(1)} %all_to_all.16.one, bf16[4,96,128]{2,1,0:T(8,128)(2,1)S(1)} %collective-permute-done.two, bf16[32,48,128]{2,1,0:T(8,128)(2,1)S(1)} %all_to_all.15.arrived), custom_call_target="tpu_custom_call" | custom-call | tf_op jit(solution)/shard_map/observe/pallas_call | solution.py:511
  46.1 19.8 %all_to_all.17.got = bf16[32,128,128]{2,1,0:T(8,128)(2,1)S(1)} all-to-all(bf16[32,128,128]{2,1,0:T(8,128)(2,1)} %observe.1), channel_id=1, replica_groups=mesh['lag_0'=4,'lag_1'=2,'lag_2'=4,'zh'=4,'core'=2] {'lag_0','lag_1','la..., dimensions={0} | all-to-all | bytes 2097152 | tf_op jit(solution)/shard_map/all_to_all | solution.py:527
  65.8 0.0 copy-start
  65.9 1.7 %collective-permute-start.1 = (bf16[32,64,128]{2,1,0:T(8,128)(2,1)S(1)}, bf16[32,64,128]{2,1,0:T(8,128)(2,1)S(1)}, u32[]{:S(2)}, u32[]{:S(2)}) collective-permute-start(bf16[32,64,128]{2,1,0:T(8,128)(2,1)S(1)} %slice.4), channel_id=1, source_target_pairs={{0,1},{1,0},{2,3},{3,2},{4,5},{5,4},{6,7},{7,6},{8,9},{9,8},{10,11... | collective-permute-start | bytes 1572872 | tf_op jit(solution)/shard_map/ppermute | solution.py:528
  67.6 1.5 %collective-permute-done.1.other = bf16[32,64,128]{2,1,0:T(8,128)(2,1)S(1)} collective-permute-done((bf16[32,64,128]{2,1,0:T(8,128)(2,1)S(1)}, bf16[32,64,128]{2,1,0:T(8,128)(2,1)S(1)}, u32[]{:S(2)}, u32[]{:S(2)}) %collective-permute-start.1) | collective-permute-done | bytes 524320 | tf_op jit(solution)/shard_map/ppermute | solution.py:528
  69.1 0.0 copy-done
  69.1 12.7 %analyse.1 = (bf16[1,128,1024]{2,1,0:T(8,128)(2,1)}, bf16[2,32,128]{2,1,0:T(8,128)(2,1)}) custom-call(s32[32]{0:T(128)} %order.5, bf16[32,128,128]{2,1,0:T(8,128)(2,1)S(1)} %all_to_all.17.got, bf16[32,64,128]{2,1,0:T(8,128)(2,1)S(1)} %collective-permute-done.1.other, bf16[1024,128]{1,0:T(8,128)(2,1)S(1)} %copy-done, f32[2,128]{1,0:T(2,128)} %variance.3), custom_call_target="tpu_custom_call" | custom-call | tf_op jit(solution)/shard_map/analyse/pallas_call | solution.py:532
  (1 shorter events, 0.0 us)
Async XLA Ops:
  2.9 17.9 %copy-start.1 = (bf16[56,128]{1,0:T(8,128)(2,1)S(1)}, bf16[56,128]{1,0:T(8,128)(2,1)}, u32[]{:S(2)}) copy-start(bf16[56,128]{1,0:T(8,128)(2,1)} %get-tuple-element.6.extra) | copy-start | bytes 43012
  36.4 5.3 %collective-permute-start = (bf16[4,96,128]{2,1,0:T(8,128)(2,1)S(1)}, bf16[4,96,128]{2,1,0:T(8,128)(2,1)S(1)}, u32[]{:S(2)}, u32[]{:S(2)}) collective-permute-start(bf16[4,96,128]{2,1,0:T(8,128)(2,1)S(1)} %all_to_all.16.one), channel_id=1, source_target_pairs={{0,1},{1,0},{2,3},{3,2},{4,5},{5,4},{6,7},{7,6},{8,9},{9,8},{10,11... | collective-permute-start | bytes 294920 | tf_op jit(solution)/shard_map/ppermute | solution.py:507
  65.8 3.3 %copy-start = (bf16[1024,128]{1,0:T(8,128)(2,1)S(1)}, bf16[1024,128]{1,0:T(8,128)(2,1)}, u32[]{:S(2)}) copy-start(bf16[1024,128]{1,0:T(8,128)(2,1)} %get-tuple-element.7.slab_t) | copy-start | bytes 786436
  65.9 3.3 %collective-permute-start.1 = (bf16[32,64,128]{2,1,0:T(8,128)(2,1)S(1)}, bf16[32,64,128]{2,1,0:T(8,128)(2,1)S(1)}, u32[]{:S(2)}, u32[]{:S(2)}) collective-permute-start(bf16[32,64,128]{2,1,0:T(8,128)(2,1)S(1)} %slice.4), channel_id=1, source_target_pairs={{0,1},{1,0},{2,3},{3,2},{4,5},{5,4},{6,7},{7,6},{8,9},{9,8},{10,11... | collective-permute-start | bytes 1572872 | tf_op jit(solution)/shard_map/ppermute | solution.py:528
